TPU v7x, 32 devices: a whole 2x2x4 slice. The times are simulated.
32 devices in a mesh: dp: 8 (over z, core), chan: 4 (over y, x).
Axes of the slice: x: 2, y: 2, z: 4, core: 2. Of those that a mesh axis runs over, the one named last changes fastest.
Arguments:
- images: bfloat16 [16, 16, 16, 2816], P('dp', None, None, 'chan'), may hold values from -6 to 6
- kernel: float32 [7, 7, 2816], P(None, None, 'chan'), may hold values from -0.875 to 0.875
- layernorm_gain: float32 [2816], P('chan'), may hold values from 0.25 to 1.75
- layernorm_bias: float32 [2816], P('chan'), may hold values from -3 to 3
- w_expand: bfloat16 [2816, 11264], P('dp', 'chan'), may hold values from -0.109375 to 0.109375
- w_reduce: bfloat16 [11264, 2816], P('chan', 'dp'), may hold values from -0.0546875 to 0.0546875
- layer_scale: float32 [2816], P('chan'), may hold values from 0.25 to 1
- cotangent: bfloat16 [16, 16, 16, 2816], P('dp', None, None, 'chan'), may hold values from -6 to 6
Outputs:
- output: bfloat16 [16, 16, 16, 2816], P('dp', None, None, 'chan')
- grad_images: bfloat16 [16, 16, 16, 2816], P('dp', None, None, 'chan')
- grad_kernel: float32 [7, 7, 2816], P(None, None, 'chan')
- gain_gradient: float32 [2816], P('chan')
- grad_bias: float32 [2816], P('chan')
- grad_expand: float32 [2816, 11264], P('dp', 'chan')
- grad_reduce: float32 [11264, 2816], P('chan', 'dp')
- grad_scale: float32 [2816], P('chan')
All inputs are finite; a program needn't handle non-finite values.
Results may differ from a plain program's by a relative error of at most 0.025.
Values may be sent and summed in bfloat16 or wider, within the bound.
A program may use at most 128 MiB of HBM per device.

v0:
```python
import math

import jax
import jax.numpy as jnp
from jax import lax
from jax.sharding import PartitionSpec as P

eps = 1e-06


def depthwise(field, kern):
    height = field.shape[1]
    breadth = field.shape[2]
    padded = jnp.pad(field, ((0, 0), (3, 3), (3, 3), (0, 0)))
    total = jnp.zeros(field.shape, jnp.float32)
    for i in range(7):
        for j in range(7):
            total = total + padded[:, i : i + height, j : j + breadth, :] * kern[i, j]
    return total


def normal_cdf(value):
    return 0.5 * (1.0 + jax.scipy.special.erf(value / math.sqrt(2.0)))


def body(
    images, kernel, layernorm_gain, layernorm_bias, w_expand, w_reduce, layer_scale, cotangent
):
    shape_in = images.shape
    height = shape_in[1]
    breadth = shape_in[2]
    positions = shape_in[0] * height * breadth
    local_chan = shape_in[3]
    image_width = local_chan * lax.axis_size("chan")
    xf = images.astype(jnp.float32)
    conv = depthwise(xf, kernel).reshape(positions, local_chan)
    mean_val = lax.psum(jnp.sum(conv, axis=1), "chan")[:, None] / image_width
    centred_rows = conv - mean_val
    var = lax.psum(jnp.sum(centred_rows * centred_rows, axis=1), "chan")[:, None] / image_width
    inverse_deviation = lax.rsqrt(var + eps)
    standardized_input = centred_rows * inverse_deviation
    normed_output = (standardized_input * layernorm_gain + layernorm_bias).astype(jnp.bfloat16)
    normed_all = lax.all_gather(normed_output, "chan", axis=1, tiled=True)
    expand_all = lax.all_gather(w_expand, "dp", axis=0, tiled=True)
    pre = jnp.dot(normed_all, expand_all, preferred_element_type=jnp.float32)
    hidden = (pre * normal_cdf(pre)).astype(jnp.bfloat16)
    reduce_all = lax.all_gather(w_reduce, "dp", axis=1, tiled=True)
    partial_branch = jnp.dot(hidden, reduce_all, preferred_element_type=jnp.float32)
    branch = lax.psum_scatter(
        partial_branch.astype(jnp.bfloat16), "chan", scatter_dimension=1, tiled=True
    ).astype(jnp.float32)
    xr = xf.reshape(positions, local_chan)
    output = (xr + layer_scale * branch).astype(jnp.bfloat16).reshape(shape_in)
    dyf = cotangent.astype(jnp.float32).reshape(positions, local_chan)
    scale_part = jnp.sum(dyf * branch, axis=0)
    dbranch = (dyf * layer_scale).astype(jnp.bfloat16)
    dbranch_all = lax.all_gather(dbranch, "chan", axis=1, tiled=True)
    dhidden = lax.dot_general(
        dbranch_all, reduce_all, (((1,), (1,)), ((), ())), preferred_element_type=jnp.float32
    )
    slope = normal_cdf(pre) + pre * jnp.exp(-0.5 * pre * pre) / math.sqrt(2.0 * math.pi)
    dpre = (dhidden * slope).astype(jnp.bfloat16)
    columns = normed_all
    grad_expand = lax.psum_scatter(
        lax.dot_general(
            columns, dpre, (((0,), (0,)), ((), ())), preferred_element_type=jnp.float32
        ).astype(jnp.bfloat16),
        "dp",
        scatter_dimension=0,
        tiled=True,
    ).astype(jnp.float32)
    partial_normed = lax.dot_general(
        dpre, expand_all, (((1,), (1,)), ((), ())), preferred_element_type=jnp.float32
    )
    normed_grad = lax.psum_scatter(
        partial_normed.astype(jnp.bfloat16), "chan", scatter_dimension=1, tiled=True
    ).astype(jnp.float32)
    columns = dbranch_all
    grad_reduce = (
        lax.psum_scatter(
            lax.dot_general(
                columns, hidden, (((0,), (0,)), ((), ())), preferred_element_type=jnp.float32
            ).astype(jnp.bfloat16),
            "dp",
            scatter_dimension=0,
            tiled=True,
        )
        .astype(jnp.float32)
        .T
    )
    gain_partial = jnp.sum(normed_grad * standardized_input, axis=0)
    bias_part = jnp.sum(normed_grad, axis=0)
    standardized_grad = normed_grad * layernorm_gain
    first_half, second_half = lax.psum(
        (
            jnp.sum(standardized_grad, axis=1),
            jnp.sum(standardized_grad * standardized_input, axis=1),
        ),
        "chan",
    )
    conv_output_grad = inverse_deviation * (
        standardized_grad
        - first_half[:, None] / image_width
        - standardized_input * (second_half[:, None] / image_width)
    )
    conv_output_grad = conv_output_grad.reshape(shape_in)
    padded = jnp.pad(xf, ((0, 0), (3, 3), (3, 3), (0, 0)))
    dpad = jnp.pad(conv_output_grad, ((0, 0), (3, 3), (3, 3), (0, 0)))
    back = cotangent.astype(jnp.float32)
    kern_rows = []
    for i in range(7):
        tap_row = []
        for j in range(7):
            tap_row.append(
                jnp.sum(
                    padded[:, i : i + height, j : j + breadth, :] * conv_output_grad, axis=(0, 1, 2)
                )
            )
            back = back + dpad[:, 6 - i : 6 - i + height, 6 - j : 6 - j + breadth, :] * kernel[i, j]
        kern_rows.append(jnp.stack(tap_row))
    kernel_part = jnp.stack(kern_rows)
    grad_images = back.astype(jnp.bfloat16)
    grad_kernel, gain_gradient, grad_bias, grad_scale = (
        lax.psum(kernel_part.astype(jnp.bfloat16), "dp").astype(jnp.float32),
        lax.psum(gain_partial.astype(jnp.bfloat16), "dp").astype(jnp.float32),
        lax.psum(bias_part.astype(jnp.bfloat16), "dp").astype(jnp.float32),
        lax.psum(scale_part.astype(jnp.bfloat16), "dp").astype(jnp.float32),
    )
    return (
        output,
        grad_images,
        grad_kernel,
        gain_gradient,
        grad_bias,
        grad_expand,
        grad_reduce,
        grad_scale,
    )


def solution(mesh):
    in_specs = (
        P("dp", None, None, "chan"),
        P(None, None, "chan"),
        P("chan"),
        P("chan"),
        P("dp", "chan"),
        P("chan", "dp"),
        P("chan"),
        P("dp", None, None, "chan"),
    )
    out_specs = (
        P("dp", None, None, "chan"),
        P("dp", None, None, "chan"),
        P(None, None, "chan"),
        P("chan"),
        P("chan"),
        P("dp", "chan"),
        P("chan", "dp"),
        P("chan"),
    )
    return jax.shard_map(body, mesh=mesh, in_specs=in_specs, out_specs=out_specs, check_vma=False)
```

profile of v0, /device:TPU:0, one launch (start us, length us, event | category | flops | bytes accessed | tf_op | source)
XLA Modules:
  0.0 969.2 jit_solution(17701858807250672959)
XLA Ops:
  7.2 1.2 slice_reduce_fusion.46
  8.4 1.4 slice_reduce_fusion.48
  9.7 1.4 slice_reduce_fusion.47
  11.2 1.3 convert_element_type.71
  12.5 12.3 %fusion.114 = (f32[2,16,16]{2,1,0:T(8,128)S(1)}, f32[2,16,16,704]{3,2,1,0:T(8,128)S(1)}) fusion(f32[704]{0:T(1024)S(1)} %get-tuple-element.115, f32[704]{0:T(1024)S(1)} %get-tuple-element.116, f32[704]{0:T(1024)S(1)} %get-tuple-element.69, f32[704]{0:T(1024)S(1)} %get-tuple-element.70, f32[704]{0:T(1024)S(1)} %get-tuple-element.71, ...), kind=kLoop, calls=%fused_computation.336 | loop fusion | flops 35323392 | bytes 3023616 | tf_op jit(solution)/shard_map/reduce_sum | solution.py:37
  24.9 11.3 %psum.56 = f32[512]{0:T(512)S(1)} all-reduce(f32[512]{0:T(512)S(1)} %reduce_sum.512), channel_id=1, replica_groups=mesh['dp'=8,'chan'=4] {'chan'}, use_global_device_ids=true, to_apply=%region_1.2 | all-reduce | flops 512 | bytes 4096 | tf_op jit(solution)/shard_map/psum | solution.py:37
  36.3 0.3 multiply_reduce_fusion.49
  36.7 8.0 psum.57
  44.7 1.9 copy.71
  46.6 1.1 add_convert_fusion
  47.8 0.7 all-gather.7.cloned.1.call-update
  48.5 0.7 all-gather.9.cloned.1.call-update
  49.2 0.6 reduce-scatter.5.cloned.1.call-start
  49.8 40.2 %all-gather.5.cloned.1.call-done = bf16[512,2816]{0,1:T(8,128)(2,1)} async-done(((bf16[512,704]{0,1:T(8,128)(2,1)}), bf16[512,2816]{0,1:T(8,128)(2,1)}) %all-gather.5.cloned.1.call-update) | async-done | bytes 2883600 | tf_op jit(solution)/shard_map/all_gather | solution.py:43
  90.0 145.3 %all-gather.7.cloned.1.call-done = bf16[2816,2816]{1,0:T(8,128)(2,1)} async-done(((bf16[352,2816]{1,0:T(8,128)(2,1)}), bf16[2816,2816]{1,0:T(8,128)(2,1)}) %all-gather.7.cloned.1.call-update) | async-done | bytes 15859728 | tf_op jit(solution)/shard_map/all_gather | solution.py:44
  235.3 15.1 %fusion.115 = f32[512,2816]{1,0:T(8,128)} fusion(bf16[512,2816]{0,1:T(8,128)(2,1)} %all-gather.5.cloned.1.call-done, bf16[2816,2816]{1,0:T(8,128)(2,1)} %all-gather.7.cloned.1.call-done), kind=kOutput, calls=%fused_computation.337 | convolution fusion | flops 8120172544 | bytes 24510464 | tf_op jit(solution)/shard_map/dot_general | solution.py:45
  250.3 128.5 %all-gather.9.cloned.1.call-done = bf16[2816,2816]{0,1:T(8,128)(2,1)} async-done(((bf16[2816,352]{0,1:T(8,128)(2,1)}), bf16[2816,2816]{0,1:T(8,128)(2,1)}) %all-gather.9.cloned.1.call-update) | async-done | bytes 15859728 | tf_op jit(solution)/shard_map/all_gather | solution.py:47
  378.8 16.3 %convolution_convert_fusion.3 = bf16[512,2816]{0,1:T(8,128)(2,1)} fusion(bf16[2816,2816]{0,1:T(8,128)(2,1)} %all-gather.9.cloned.1.call-done, f32[512,2816]{1,0:T(8,128)} %fusion.115), kind=kOutput, calls=%fused_computation.108 | convolution fusion | flops 8128823296 | bytes 24510464 | tf_op jit(solution)/shard_map/dot_general | solution.py:48
  395.1 2.5 copy.74
  397.6 1.6 copy.72
  399.3 36.0 %reduce-scatter.5.cloned.1.call-done = bf16[512,704]{0,1:T(8,128)(2,1)} async-done(((bf16[512,2816]{0,1:T(8,128)(2,1)}), bf16[512,704]{0,1:T(8,128)(2,1)}) %reduce-scatter.5.cloned.1.call-update) | async-done | bytes 720912 | tf_op jit(solution)/shard_map/reduce_scatter | solution.py:49
  435.2 3.5 fusion.109
  439.0 41.7 %all-gather.11.cloned.1.call-done = bf16[512,2816]{0,1:T(8,128)(2,1)} async-done(((bf16[512,704]{0,1:T(8,128)(2,1)}), bf16[512,2816]{0,1:T(8,128)(2,1)}) %all-gather.11.cloned.1.call-update) | async-done | bytes 2883600 | tf_op jit(solution)/shard_map/all_gather | solution.py:57
  480.7 16.1 %fusion.5 = bf16[512,2816]{1,0:T(8,128)(2,1)S(1)} fusion(f32[512,2816]{1,0:T(8,128)} %fusion.115, bf16[512,2816]{0,1:T(8,128)(2,1)} %all-gather.11.cloned.1.call-done, bf16[2816,2816]{0,1:T(8,128)(2,1)} %all-gather.9.cloned.1.call-done), kind=kOutput, calls=%fused_computation.104 | convolution fusion | flops 8134590464 | bytes 27394048 | tf_op jit(solution)/shard_map/dot_general | solution.py:58
  496.8 1.6 copy-done.7
  498.4 13.0 %convolution_convert_fusion.2 = bf16[512,2816]{0,1:T(8,128)(2,1)} fusion(bf16[512,2816]{1,0:T(8,128)(2,1)S(1)} %fusion.5, bf16[2816,2816]{1,0:T(8,128)(2,1)} %all-gather.7.cloned.1.call-done), kind=kOutput, calls=%fused_computation.107 | convolution fusion | flops 8121614336 | bytes 21626880 | tf_op jit(solution)/shard_map/dot_general | solution.py:72
  511.4 41.8 %reduce-scatter.7.cloned.1.call-done = bf16[512,704]{0,1:T(8,128)(2,1)} async-done(((bf16[512,2816]{0,1:T(8,128)(2,1)}), bf16[512,704]{0,1:T(8,128)(2,1)}) %reduce-scatter.7.cloned.1.call-update) | async-done | bytes 720912 | tf_op jit(solution)/shard_map/reduce_scatter | solution.py:75
  553.3 1.7 fusion.113
  555.0 9.1 all-reduce.2
  564.1 2.6 fusion.111
  566.8 1.8 copy.75
  568.6 3.8 multiply_reduce_fusion.2
  572.4 4.2 multiply_reduce_fusion
  576.7 4.5 multiply_reduce_fusion.1
  582.2 0.6 copy-done.3
  582.9 15.4 %convolution_convert_fusion = bf16[2816,2816]{1,0:T(8,128)(2,1)} fusion(bf16[512,2816]{0,1:T(8,128)(2,1)} %all-gather.11.cloned.1.call-done, f32[512,2816]{1,0:T(8,128)} %fusion.115), kind=kOutput, calls=%fused_computation.96 | convolution fusion | flops 8135311360 | bytes 24510464 | tf_op jit(solution)/shard_map/dot_general | solution.py:81
  598.7 13.9 %convolution_convert_fusion.1 = bf16[2816,2816]{1,0:T(8,128)(2,1)} fusion(bf16[512,2816]{0,1:T(8,128)(2,1)} %all-gather.5.cloned.1.call-done, bf16[512,2816]{1,0:T(8,128)(2,1)} %copy-done.7), kind=kOutput, calls=%fused_computation.97 | convolution fusion | flops 8128102400 | bytes 21626880 | tf_op jit(solution)/shard_map/dot_general | solution.py:65
  612.6 2.4 copy.73
  615.2 14.6 %all-reduce.3 = (bf16[704]{0:T(1024)(128)(2,1)S(1)}, bf16[704]{0:T(1024)(128)(2,1)S(1)}, bf16[704]{0:T(1024)(128)(2,1)S(1)}) all-reduce(bf16[704]{0:T(1024)(128)(2,1)S(1)} %get-tuple-element.64, bf16[704]{0:T(1024)(128)(2,1)S(1)} %reduce_sum.567, bf16[704]{0:T(1024)(128)(2,1)S(1)} %get-tuple-element.124), channel_id=1, replica_groups=mesh['dp'=8,'chan'=4] {'dp'}, use_global_device_ids=true, to_apply=%region_61.62 | all-reduce | flops 2112 | bytes 8448 | tf_op jit(solution)/shard_map/psum | solution.py:125
  629.8 0.6 convert_element_type.85
  630.4 0.6 convert_element_type.86
  631.0 0.6 convert_element_type.91
  631.6 12.3 %fusion.102 = bf16[2,16,16,704]{3,2,1,0:T(8,128)(2,1)} fusion(f32[2,16,16,704]{3,2,1,0:T(8,128)S(1)} %bitcast.82, f32[704]{0:T(1024)S(1)} %get-tuple-element.115, f32[704]{0:T(1024)S(1)} %get-tuple-element.116, f32[704]{0:T(1024)S(1)} %get-tuple-element.69, f32[704]{0:T(1024)S(1)} %get-tuple-element.70, f32[704]{0:T(1024)S(1)} %get-tuple-element.71, ...), kind=kLoop, calls=%fused_computation.210 | loop fusion | flops 36044800 | bytes 3021568 | tf_op jit(solution)/shard_map/convert_element_type | solution.py:122
  643.9 1.6 convert_element_type.83
  645.5 152.7 %reduce-scatter.11.cloned.1.call-done = bf16[352,2816]{1,0:T(8,128)(2,1)} async-done(((bf16[2816,2816]{1,0:T(8,128)(2,1)}), bf16[352,2816]{1,0:T(8,128)(2,1)}) %reduce-scatter.11.cloned.1.call-update) | async-done | bytes 1982480 | tf_op jit(solution)/shard_map/reduce_scatter | solution.py:80
  798.2 3.7 convert_bitcast_fusion
  802.0 156.8 %reduce-scatter.9.cloned.1.call-done = bf16[352,2816]{1,0:T(8,128)(2,1)} async-done(((bf16[2816,2816]{1,0:T(8,128)(2,1)}), bf16[352,2816]{1,0:T(8,128)(2,1)}) %reduce-scatter.9.cloned.1.call-update) | async-done | bytes 1982480 | tf_op jit(solution)/shard_map/reduce_scatter | solution.py:64
  958.7 3.7 convert_element_type.88
  (100 shorter events, 2.0 us)
Async XLA Ops:
  7.2 82.8 %all-gather.5.cloned.1.call-start = ((), (), s32[]{:S(2)}) async-start(), calls=%async_computation.4 | async-start | bytes 3604480 | tf_op jit(solution)/shard_map/all_gather | solution.py:43
  24.8 19.9 %copy-start = (f32[2,16,16,704]{3,2,1,0:T(8,128)}, f32[2,16,16,704]{3,2,1,0:T(8,128)S(1)}, u32[]{:S(2)}) copy-start(f32[2,16,16,704]{3,2,1,0:T(8,128)S(1)} %get-tuple-element.123) | copy-start | bytes 4325380
  36.6 9.9 %copy-start.4 = (f32[704]{0:T(1024)S(1)}, f32[704]{0:T(1024)}, u32[]{:S(2)}) copy-start(f32[704]{0:T(1024)} %param.10) | copy-start | bytes 8452
  36.6 9.9 %copy-start.5 = (f32[704]{0:T(1024)S(1)}, f32[704]{0:T(1024)}, u32[]{:S(2)}) copy-start(f32[704]{0:T(1024)} %param.11) | copy-start | bytes 8452
  47.7 187.5 %all-gather.7.cloned.1.call-start = ((), (), s32[]{:S(2)}) async-start(), calls=%async_computation.5 | async-start | bytes 17842176 | tf_op jit(solution)/shard_map/all_gather | solution.py:44
  48.5 330.3 %all-gather.9.cloned.1.call-start = ((), (), s32[]{:S(2)}) async-start(), calls=%async_computation.6 | async-start | bytes 17842176 | tf_op jit(solution)/shard_map/all_gather | solution.py:47
  49.2 386.0 %reduce-scatter.5.cloned.1.call-start = ((), (), s32[]{:S(2)}) async-start(), calls=%async_computation.7 | async-start | bytes 3604480 | tf_op jit(solution)/shard_map/reduce_scatter | solution.py:49
  395.1 85.6 %all-gather.11.cloned.1.call-start = ((), (), s32[]{:S(2)}) async-start(), calls=%async_computation.8 | async-start | bytes 3604480 | tf_op jit(solution)/shard_map/all_gather | solution.py:57
  397.6 37.6 %copy-start.6 = (f32[704]{0:T(1024)S(1)}, f32[704]{0:T(1024)}, u32[]{:S(2)}) copy-start(f32[704]{0:T(1024)} %param.14) | copy-start | bytes 8452
  438.8 114.5 %reduce-scatter.7.cloned.1.call-start = ((), (), s32[]{:S(2)}) async-start(), calls=%async_computation.9 | async-start | bytes 3604480 | tf_op jit(solution)/shard_map/reduce_scatter | solution.py:75
  496.8 1.6 copy-start.7
  511.4 132.5 %all-reduce.6.cloned.1.call-start = ((), (), s32[]{:S(2)}) async-start(), calls=%async_computation.10 | async-start | bytes 172032 | tf_op jit(solution)/shard_map/psum | solution.py:124
  582.2 0.6 copy-start.3
  582.9 215.4 %reduce-scatter.11.cloned.1.call-start = ((), (), s32[]{:S(2)}) async-start(), calls=%async_computation.12 | async-start | bytes 17842176 | tf_op jit(solution)/shard_map/reduce_scatter | solution.py:80
  598.4 360.3 %reduce-scatter.9.cloned.1.call-start = ((), (), s32[]{:S(2)}) async-start(), calls=%async_computation.11 | async-start | bytes 17842176 | tf_op jit(solution)/shard_map/reduce_scatter | solution.py:64
  612.6 2.4 copy-start.1
  612.6 19.0 %copy-start.2 = (bf16[2,16,16,704]{3,2,1,0:T(8,128)(2,1)S(1)}, bf16[2,16,16,704]{3,2,1,0:T(8,128)(2,1)}, u32[]{:S(2)}) copy-start(bf16[2,16,16,704]{3,2,1,0:T(8,128)(2,1)} %param.15) | copy-start | bytes 2162692
Sparse Core Ops, SparseCore 0:
  47.9 42.1 all-gather.4
  91.7 143.5 all-gather.6
  236.9 141.8 all-gather.8
  395.2 39.9 reduce-scatter.4
  438.9 41.7 all-gather.10
  511.5 41.7 reduce-scatter.6
  583.0 50.0 all-reduce.5
  635.5 162.6 reduce-scatter.10
  800.7 157.9 reduce-scatter.8
where the time goes:
time: 974 us; the launch traced here: 969 us
  waiting for transfers between devices  744 us (76%)
  matrix products  89.7 us (9%)
  other arithmetic  58.8 us (6%)
  blocking collectives  43 us (4%)
  local copies, waits for them, and re-layouts  17.3 us (2%)
  between operations  14.7 us (2%)
    reduce_scatter x1, waiting for transfers between devices, body(): lax.psum_scatter(lax.dot_general(columns, dpre, (((0,), (0,)), ((), ())),...  157 us
    reduce_scatter x1, waiting for transfers between devices, body(): lax.psum_scatter(lax.dot_general(columns, hidden, (((0,), (0,)), ((), ())...  153 us
    all_gather x1, waiting for transfers between devices, body(): expand_all = lax.all_gather(w_expand, 'dp', axis=0, tiled=True)  145 us
    all_gather x1, waiting for transfers between devices, body(): reduce_all = lax.all_gather(w_reduce, 'dp', axis=1, tiled=True)  128 us
    reduce_scatter x1, waiting for transfers between devices, body(): lax.psum_scatter(partial_normed.astype(jnp.bfloat16), 'chan', scatter_dim...  41.8 us
    all_gather x1, waiting for transfers between devices, body(): dbranch_all = lax.all_gather(dbranch, 'chan', axis=1, tiled=True)  41.7 us
    all_gather x1, waiting for transfers between devices, body(): normed_all = lax.all_gather(normed_output, 'chan', axis=1, tiled=True)  40.2 us
    reduce_scatter x1, waiting for transfers between devices, body(): lax.psum_scatter(partial_branch.astype(jnp.bfloat16), 'chan', scatter_dim...  36 us
  transfers between devices with their start and end apart: 9, of which 8 were waited for; matrix products, arithmetic and copies ran while one was open for 7% of the time, Pallas kernels for 0%

commit v1 on v0

--- a/solution.py
+++ b/solution.py
@@ -23,6 +23,45 @@
     return 0.5 * (1.0 + jax.scipy.special.erf(value / math.sqrt(2.0)))
 
 
+def swap_pairs(shift, n):
+    return [(i, i ^ shift) for i in range(n)]
+
+
+def chan_gather(block):
+    n = lax.axis_size("chan")
+    me = lax.axis_index("chan")
+    width = block.shape[1]
+    whole = jnp.zeros((block.shape[0], n * width), block.dtype)
+    parts = [block] + [lax.ppermute(block, "chan", swap_pairs(k, n)) for k in range(1, n)]
+    for k in range(n):
+        whole = lax.dynamic_update_slice(whole, parts[k], (0, (me ^ k) * width))
+    return whole
+
+
+def chan_scatter(partial):
+    n = lax.axis_size("chan")
+    me = lax.axis_index("chan")
+    width = partial.shape[1] // n
+    total = lax.dynamic_slice_in_dim(partial, me * width, width, 1).astype(jnp.float32)
+    for k in range(1, n):
+        mine = lax.dynamic_slice_in_dim(partial, (me ^ k) * width, width, 1)
+        total = total + lax.ppermute(mine, "chan", swap_pairs(k, n)).astype(jnp.float32)
+    return total
+
+
+def dp_scatter(partial):
+    return lax.psum_scatter(partial, "dp", scatter_dimension=0, tiled=True)
+
+
+def dp_total(value):
+    n = lax.axis_size("dp")
+    shift = 1
+    while shift < n:
+        value = value + lax.ppermute(value, "dp", swap_pairs(shift, n))
+        shift *= 2
+    return value
+
+
 def body(
     images, kernel, layernorm_gain, layernorm_bias, w_expand, w_reduce, layer_scale, cotangent
 ):
@@ -40,54 +79,40 @@
     inverse_deviation = lax.rsqrt(var + eps)
     standardized_input = centred_rows * inverse_deviation
     normed_output = (standardized_input * layernorm_gain + layernorm_bias).astype(jnp.bfloat16)
-    normed_all = lax.all_gather(normed_output, "chan", axis=1, tiled=True)
+    normed_all = chan_gather(normed_output)
     expand_all = lax.all_gather(w_expand, "dp", axis=0, tiled=True)
     pre = jnp.dot(normed_all, expand_all, preferred_element_type=jnp.float32)
     hidden = (pre * normal_cdf(pre)).astype(jnp.bfloat16)
+    dyf = cotangent.astype(jnp.float32).reshape(positions, local_chan)
+    dbranch = (dyf * layer_scale).astype(jnp.bfloat16)
+    dbranch_all = chan_gather(dbranch)
+    reduce_part = lax.dot_general(
+        dbranch_all, hidden, (((0,), (0,)), ((), ())), preferred_element_type=jnp.float32
+    ).astype(jnp.bfloat16)
     reduce_all = lax.all_gather(w_reduce, "dp", axis=1, tiled=True)
-    partial_branch = jnp.dot(hidden, reduce_all, preferred_element_type=jnp.float32)
-    branch = lax.psum_scatter(
-        partial_branch.astype(jnp.bfloat16), "chan", scatter_dimension=1, tiled=True
-    ).astype(jnp.float32)
-    xr = xf.reshape(positions, local_chan)
-    output = (xr + layer_scale * branch).astype(jnp.bfloat16).reshape(shape_in)
-    dyf = cotangent.astype(jnp.float32).reshape(positions, local_chan)
-    scale_part = jnp.sum(dyf * branch, axis=0)
-    dbranch = (dyf * layer_scale).astype(jnp.bfloat16)
-    dbranch_all = lax.all_gather(dbranch, "chan", axis=1, tiled=True)
+    reduce_part, reduce_all = lax.optimization_barrier((reduce_part, reduce_all))
+    grad_reduce = dp_scatter(reduce_part).astype(jnp.float32).T
     dhidden = lax.dot_general(
         dbranch_all, reduce_all, (((1,), (1,)), ((), ())), preferred_element_type=jnp.float32
     )
     slope = normal_cdf(pre) + pre * jnp.exp(-0.5 * pre * pre) / math.sqrt(2.0 * math.pi)
     dpre = (dhidden * slope).astype(jnp.bfloat16)
-    columns = normed_all
-    grad_expand = lax.psum_scatter(
-        lax.dot_general(
-            columns, dpre, (((0,), (0,)), ((), ())), preferred_element_type=jnp.float32
-        ).astype(jnp.bfloat16),
-        "dp",
-        scatter_dimension=0,
-        tiled=True,
-    ).astype(jnp.float32)
+    expand_part = lax.dot_general(
+        normed_all, dpre, (((0,), (0,)), ((), ())), preferred_element_type=jnp.float32
+    ).astype(jnp.bfloat16)
+    expand_part, dpre, hidden, reduce_all = lax.optimization_barrier(
+        (expand_part, dpre, hidden, reduce_all)
+    )
+    grad_expand = dp_scatter(expand_part).astype(jnp.float32)
     partial_normed = lax.dot_general(
         dpre, expand_all, (((1,), (1,)), ((), ())), preferred_element_type=jnp.float32
     )
-    normed_grad = lax.psum_scatter(
-        partial_normed.astype(jnp.bfloat16), "chan", scatter_dimension=1, tiled=True
-    ).astype(jnp.float32)
-    columns = dbranch_all
-    grad_reduce = (
-        lax.psum_scatter(
-            lax.dot_general(
-                columns, hidden, (((0,), (0,)), ((), ())), preferred_element_type=jnp.float32
-            ).astype(jnp.bfloat16),
-            "dp",
-            scatter_dimension=0,
-            tiled=True,
-        )
-        .astype(jnp.float32)
-        .T
-    )
+    normed_grad = chan_scatter(partial_normed.astype(jnp.bfloat16))
+    partial_branch = jnp.dot(hidden, reduce_all, preferred_element_type=jnp.float32)
+    branch = chan_scatter(partial_branch.astype(jnp.bfloat16))
+    xr = xf.reshape(positions, local_chan)
+    output = (xr + layer_scale * branch).astype(jnp.bfloat16).reshape(shape_in)
+    scale_part = jnp.sum(dyf * branch, axis=0)
     gain_partial = jnp.sum(normed_grad * standardized_input, axis=0)
     bias_part = jnp.sum(normed_grad, axis=0)
     standardized_grad = normed_grad * layernorm_gain
@@ -120,12 +145,19 @@
         kern_rows.append(jnp.stack(tap_row))
     kernel_part = jnp.stack(kern_rows)
     grad_images = back.astype(jnp.bfloat16)
-    grad_kernel, gain_gradient, grad_bias, grad_scale = (
-        lax.psum(kernel_part.astype(jnp.bfloat16), "dp").astype(jnp.float32),
-        lax.psum(gain_partial.astype(jnp.bfloat16), "dp").astype(jnp.float32),
-        lax.psum(bias_part.astype(jnp.bfloat16), "dp").astype(jnp.float32),
-        lax.psum(scale_part.astype(jnp.bfloat16), "dp").astype(jnp.float32),
+    small = dp_total(
+        jnp.concatenate(
+            [
+                kernel_part.reshape(-1, local_chan),
+                gain_partial[None],
+                bias_part[None],
+                scale_part[None],
+            ]
+        )
     )
+    taps = kernel_part.shape[0] * kernel_part.shape[1]
+    grad_kernel = small[:taps].reshape(kernel_part.shape)
+    gain_gradient, grad_bias, grad_scale = small[taps], small[taps + 1], small[taps + 2]
     return (
         output,
         grad_images,

time: 974 us -> 644 us (0.66)
  waiting for transfers between devices: 744 us -> 307 us
  local copies, waits for them, and re-layouts: 17.3 us -> 128 us
  starting transfers between devices: 1.31 us -> 16.4 us
  blocking collectives: 43 us -> 29.3 us
    reduce_scatter x4 -> x2, waiting for transfers between devices: 387 us -> 142 us  [dp_scatter(): return lax.psum_scatter(partial, 'dp', scatter_dimension=0, tiled=True)]
    all_gather x1, waiting for transfers between devices: 145 us -> 5.22 us  [body(): expand_all = lax.all_gather(w_expand, 'dp', axis=0, tiled=True)]
    all_gather x2 -> x0, waiting for transfers between devices: 81.9 us -> none  [the longest x1 41.7 us: body(): dbranch_all = lax.all_gather(dbranch, 'chan', axis=1, tiled=True)]
    dynamic_update_slice x0 -> x8, local copies, waits for them, and re-layouts: none -> 67.1 us  [chan_gather(): whole = lax.dynamic_update_slice(whole, parts[k], (0, (me ^ k) * width))]
    ppermute x0 -> x15, waiting for transfers between devices: none -> 44.2 us  [the longest x6 26.9 us: chan_scatter(): lax.ppermute(mine, 'chan', swap_pairs(k, n)).astype(jnp.float32)]
    ppermute x0 -> x12, local copies, waits for them, and re-layouts: none -> 27.4 us  [the longest x6 13.8 us: chan_scatter(): lax.ppermute(mine, 'chan', swap_pairs(k, n)).astype(jnp.float32)]
    dynamic_slice x0 -> x8, local copies, waits for them, and re-layouts: none -> 19.2 us  [chan_scatter(): mine = lax.dynamic_slice_in_dim(partial, (me ^ k) * width, width, 1)]
    ppermute x0 -> x15, starting transfers between devices: none -> 16.3 us  [the longest x6 7.91 us: chan_scatter(): lax.ppermute(mine, 'chan', swap_pairs(k, n)).astype(jnp.float32)]
  transfers between devices with their start and end apart: 9 -> 19, of which waited for: 8 -> 8; matrix products, arithmetic and copies ran while one was open for 7% -> 41% of each run, Pallas kernels for 0% -> 0%
where the time goes in v1:
time: 644 us; the launch traced here: 633 us
  waiting for transfers between devices  307 us (48%)
  local copies, waits for them, and re-layouts  128 us (20%)
  matrix products  81.8 us (13%)
  other arithmetic  54.9 us (9%)
  blocking collectives  29.3 us (5%)
  starting transfers between devices  16.4 us (3%)
  between operations  15 us (2%)
    reduce_scatter x2, waiting for transfers between devices, dp_scatter(): return lax.psum_scatter(partial, 'dp', scatter_dimension=0, tiled=True)  142 us
    all_gather x1, waiting for transfers between devices, body(): reduce_all = lax.all_gather(w_reduce, 'dp', axis=1, tiled=True)  115 us
    dynamic_update_slice x8, local copies, waits for them, and re-layouts, chan_gather(): whole = lax.dynamic_update_slice(whole, parts[k], (0, (me ^ k) * width))  67.1 us
    ppermute x6, waiting for transfers between devices, chan_scatter(): lax.ppermute(mine, 'chan', swap_pairs(k, n)).astype(jnp.float32)  26.9 us
    dynamic_slice x8, local copies, waits for them, and re-layouts, chan_scatter(): mine = lax.dynamic_slice_in_dim(partial, (me ^ k) * width, width, 1)  19.2 us
    dot_general x1, matrix products, body(): lax.dot_general(dbranch_all, reduce_all, (((1,), (1,)), ((), ())), prefer...  15.3 us
    dot_general x1, matrix products, body(): pre = jnp.dot(normed_all, expand_all, preferred_element_type=jnp.float32)  15.2 us
    ppermute x6, local copies, waits for them, and re-layouts, chan_scatter(): lax.ppermute(mine, 'chan', swap_pairs(k, n)).astype(jnp.float32)  13.8 us
  transfers between devices with their start and end apart: 19, of which 8 were waited for; matrix products, arithmetic and copies ran while one was open for 41% of the time, Pallas kernels for 0%

profile of v1, /device:TPU:0, one launch (start us, length us, event | category | flops | bytes accessed | tf_op | source)
XLA Modules:
  0.0 632.6 jit_solution(10809469362754886029)
XLA Ops:
  10.0 12.3 %fusion.108 = (f32[2,16,16]{2,1,0:T(8,128)S(1)}, f32[2,16,16,704]{3,2,1,0:T(8,128)S(1)}) fusion(f32[704]{0:T(1024)S(1)} %get-tuple-element.123, f32[704]{0:T(1024)S(1)} %get-tuple-element.124, f32[704]{0:T(1024)S(1)} %get-tuple-element.77, f32[704]{0:T(1024)S(1)} %get-tuple-element.78, f32[704]{0:T(1024)S(1)} %get-tuple-element.79, ...), kind=kLoop, calls=%fused_computation.344 | loop fusion | flops 35323392 | bytes 3023616 | tf_op jit(solution)/shard_map/reduce_sum | solution.py:76
  22.4 11.3 %psum.28 = f32[512]{0:T(512)S(1)} all-reduce(f32[512]{0:T(512)S(1)} %reduce_sum.509), channel_id=1, replica_groups=mesh['dp'=8,'chan'=4] {'chan'}, use_global_device_ids=true, to_apply=%region_1.2 | all-reduce | flops 512 | bytes 4096 | tf_op jit(solution)/shard_map/psum | solution.py:76
  34.2 7.9 %psum.29 = f32[512]{0:T(512)S(1)} all-reduce(f32[512]{0:T(512)S(1)} %reduce_sum.511), channel_id=1, replica_groups=mesh['dp'=8,'chan'=4] {'chan'}, use_global_device_ids=true, to_apply=%region_3.4 | all-reduce | flops 512 | bytes 4096 | tf_op jit(solution)/shard_map/psum | solution.py:78
  49.2 2.3 copy.22
  55.7 9.3 %collective-permute-done = bf16[512,704]{0,1:T(8,128)(2,1)} collective-permute-done((bf16[512,704]{0,1:T(8,128)(2,1)}, bf16[512,704]{0,1:T(8,128)(2,1)}, u32[]{:S(2)}, u32[]{:S(2)}) %collective-permute-start) | collective-permute-done | bytes 720928 | tf_op jit(solution)/shard_map/ppermute | solution.py:35
  68.3 8.1 %dynamic_update_slice.24 = bf16[512,2816]{1,0:T(8,128)(2,1)} dynamic-update-slice(bf16[512,2816]{1,0:T(8,128)(2,1)} %broadcast.39.clone, bf16[512,704]{1,0:T(8,128)(2,1)} %add_convert_fusion, s32[]{:T(128)} %constant.11.clone.1, s32[]{:T(128)S(6)} %select_n.8) | dynamic-update-slice | bytes 1441796 | tf_op jit(solution)/shard_map/dynamic_update_slice | solution.py:37
  78.2 8.1 %dynamic_update_slice.28 = bf16[512,2816]{1,0:T(8,128)(2,1)} dynamic-update-slice(bf16[512,2816]{1,0:T(8,128)(2,1)} %broadcast.39.clone.1, bf16[512,704]{1,0:T(8,128)(2,1)} %fusion.104, s32[]{:T(128)} %constant.11.clone.1, s32[]{:T(128)S(6)} %select_n.8) | dynamic-update-slice | bytes 1441796 | tf_op jit(solution)/shard_map/dynamic_update_slice | solution.py:37
  88.6 9.0 %dynamic_update_slice.25 = bf16[512,2816]{1,0:T(8,128)(2,1)} dynamic-update-slice(bf16[512,2816]{1,0:T(8,128)(2,1)} %dynamic_update_slice.24, bf16[512,704]{1,0:T(8,128)(2,1)} %copy.17, s32[]{:T(128)} %constant.11.clone.1, s32[]{:T(128)S(6)} %select_n.9) | dynamic-update-slice | bytes 1441796 | tf_op jit(solution)/shard_map/dynamic_update_slice | solution.py:37
  97.6 2.3 copy.23
  99.8 9.0 %dynamic_update_slice.29 = bf16[512,2816]{1,0:T(8,128)(2,1)} dynamic-update-slice(bf16[512,2816]{1,0:T(8,128)(2,1)} %dynamic_update_slice.28, bf16[512,704]{1,0:T(8,128)(2,1)} %copy.23, s32[]{:T(128)} %constant.11.clone.1, s32[]{:T(128)S(6)} %select_n.9) | dynamic-update-slice | bytes 1441796 | tf_op jit(solution)/shard_map/dynamic_update_slice | solution.py:37
  111.1 8.1 %dynamic_update_slice.26 = bf16[512,2816]{1,0:T(8,128)(2,1)} dynamic-update-slice(bf16[512,2816]{1,0:T(8,128)(2,1)} %dynamic_update_slice.25, bf16[512,704]{1,0:T(8,128)(2,1)} %copy.19, s32[]{:T(128)} %constant.11.clone.1, s32[]{:T(128)S(6)} %select_n.10) | dynamic-update-slice | bytes 1441796 | tf_op jit(solution)/shard_map/dynamic_update_slice | solution.py:37
  121.4 8.1 %dynamic_update_slice.30 = bf16[512,2816]{1,0:T(8,128)(2,1)} dynamic-update-slice(bf16[512,2816]{1,0:T(8,128)(2,1)} %dynamic_update_slice.29, bf16[512,704]{1,0:T(8,128)(2,1)} %copy.25, s32[]{:T(128)} %constant.11.clone.1, s32[]{:T(128)S(6)} %select_n.10) | dynamic-update-slice | bytes 1441796 | tf_op jit(solution)/shard_map/dynamic_update_slice | solution.py:37
  131.8 8.3 %dynamic_update_slice.27 = bf16[512,2816]{1,0:T(8,128)(2,1)} dynamic-update-slice(bf16[512,2816]{1,0:T(8,128)(2,1)} %dynamic_update_slice.26, bf16[512,704]{1,0:T(8,128)(2,1)} %copy.21, s32[]{:T(128)} %constant.11.clone.1, s32[]{:T(128)S(6)} %select_n.11) | dynamic-update-slice | bytes 1441796 | tf_op jit(solution)/shard_map/dynamic_update_slice | solution.py:37
  140.1 2.3 copy.27
  142.4 8.3 %dynamic_update_slice.31 = bf16[512,2816]{1,0:T(8,128)(2,1)} dynamic-update-slice(bf16[512,2816]{1,0:T(8,128)(2,1)} %dynamic_update_slice.30, bf16[512,704]{1,0:T(8,128)(2,1)} %copy.27, s32[]{:T(128)} %constant.11.clone.1, s32[]{:T(128)S(6)} %select_n.11) | dynamic-update-slice | bytes 1441796 | tf_op jit(solution)/shard_map/dynamic_update_slice | solution.py:37
  150.8 5.2 all-gather.3.cloned.1.call-done
  156.0 15.2 %multiply_convert_fusion = (bf16[512,2816]{1,0:T(8,128)(2,1)S(1)}, f32[512,2816]{1,0:T(8,128)}) fusion(bf16[512,2816]{1,0:T(8,128)(2,1)} %dynamic_update_slice.27, bf16[2816,2816]{1,0:T(8,128)(2,1)} %all-gather.3.cloned.1.call-done), kind=kOutput, calls=%fused_computation.105 | convolution fusion | flops 8127381504 | bytes 27394048 | tf_op jit(solution)/shard_map/dot_general | solution.py:84
  172.8 12.1 %convolution_convert_fusion.1 = bf16[2816,2816]{1,0:T(8,128)(2,1)} fusion(bf16[512,2816]{1,0:T(8,128)(2,1)S(1)} %copy-done.7, bf16[512,2816]{1,0:T(8,128)(2,1)S(1)} %get-tuple-element.15), kind=kOutput, calls=%fused_computation.97 | convolution fusion | flops 8128102400 | bytes 21626880 | tf_op jit(solution)/shard_map/dot_general | solution.py:89
  184.9 114.6 %all-gather.5.cloned.1.call-done = bf16[2816,2816]{0,1:T(8,128)(2,1)} async-done(((bf16[2816,352]{0,1:T(8,128)(2,1)}), bf16[2816,2816]{0,1:T(8,128)(2,1)}) %all-gather.5.cloned.1.call-update) | async-done | bytes 15859728 | tf_op jit(solution)/shard_map/all_gather | solution.py:92
  299.6 15.3 %fusion.5 = bf16[512,2816]{1,0:T(8,128)(2,1)S(1)} fusion(f32[512,2816]{1,0:T(8,128)} %get-tuple-element.140, bf16[512,2816]{1,0:T(8,128)(2,1)} %dynamic_update_slice.31, bf16[2816,2816]{0,1:T(8,128)(2,1)} %all-gather.5.cloned.1.call-done), kind=kOutput, calls=%fused_computation.104 | convolution fusion | flops 8134590464 | bytes 27394048 | tf_op jit(solution)/shard_map/dot_general | solution.py:95
  316.4 11.9 %convolution_convert_fusion = bf16[2816,2816]{1,0:T(8,128)(2,1)} fusion(bf16[512,2816]{1,0:T(8,128)(2,1)S(1)} %copy-done.8, bf16[512,2816]{1,0:T(8,128)(2,1)S(1)} %fusion.5), kind=kOutput, calls=%fused_computation.96 | convolution fusion | flops 8128102400 | bytes 21626880 | tf_op jit(solution)/shard_map/dot_general | solution.py:100
  328.3 13.7 %convolution_convert_fusion.3 = bf16[512,2816]{1,0:T(8,128)(2,1)S(1)} fusion(bf16[512,2816]{1,0:T(8,128)(2,1)} %copy-done.13, bf16[2816,2816]{0,1:T(8,128)(2,1)} %all-gather.5.cloned.1.call-done), kind=kOutput, calls=%fused_computation.108 | convolution fusion | flops 8121614336 | bytes 21626880 | tf_op jit(solution)/shard_map/dot_general | solution.py:111
  342.1 2.8 constant_dynamic-slice_fusion.5
  344.9 2.3 copy.28
  347.2 2.3 copy.32
  355.2 13.5 %convolution_convert_fusion.2 = bf16[512,2816]{1,0:T(8,128)(2,1)S(1)} fusion(bf16[512,2816]{1,0:T(8,128)(2,1)} %copy-done.14, bf16[2816,2816]{1,0:T(8,128)(2,1)} %all-gather.3.cloned.1.call-done), kind=kOutput, calls=%fused_computation.107 | convolution fusion | flops 8121614336 | bytes 21626880 | tf_op jit(solution)/shard_map/dot_general | solution.py:107
  368.8 2.8 constant_dynamic-slice_fusion.2
  371.5 2.3 copy.34
  373.8 2.3 copy.36
  377.6 2.3 copy.38
  381.4 5.1 collective-permute-done.7
  387.9 2.3 copy.31
  390.2 2.3 copy.33
  392.5 2.3 copy.29
  394.8 21.8 %collective-permute-done.10 = bf16[512,704]{0,1:T(8,128)(2,1)} collective-permute-done((bf16[512,704]{0,1:T(8,128)(2,1)}, bf16[512,704]{0,1:T(8,128)(2,1)}, u32[]{:S(2)}, u32[]{:S(2)}) %collective-permute-start.10) | collective-permute-done | bytes 720928 | tf_op jit(solution)/shard_map/ppermute | solution.py:48
  416.6 2.3 copy.37
  418.9 2.3 copy.39
  421.3 2.3 copy.35
  423.5 5.4 fusion.105
  429.0 10.0 %all-reduce.2 = (f32[512]{0:T(512)S(1)}, f32[512]{0:T(512)S(1)}) all-reduce(f32[512]{0:T(512)S(1)} %get-tuple-element.143, f32[512]{0:T(512)S(1)} %get-tuple-element.142), channel_id=1, replica_groups=mesh['dp'=8,'chan'=4] {'chan'}, use_global_device_ids=true, to_apply=%region_7.8 | all-reduce | flops 1024 | bytes 8192 | tf_op jit(solution)/shard_map/psum | solution.py:119
  439.0 6.5 %multiply_reduce_fusion.2 = (f32[704]{0:T(1024)S(1)}, f32[704]{0:T(1024)S(1)}, f32[704]{0:T(1024)S(1)}, f32[704]{0:T(1024)S(1)}, f32[704]{0:T(1024)S(1)}, /*inde...) fusion(f32[2,16,16,704]{3,2,1,0:T(8,128)S(1)} %convert_element_, ...), kind=kLoop, calls=%fused_computation.218 | loop fusion | flops 15486592 | bytes 5828864 | tf_op jit(solution)/shard_map/reduce_sum | solution.py:140
  445.7 4.1 multiply_reduce_fusion.1
  449.9 2.8 multiply_reduce_fusion.3
  455.2 6.6 %collective-permute-done.13 = f32[52,704]{1,0:T(8,128)S(1)} collective-permute-done((f32[52,704]{1,0:T(8,128)S(1)}, f32[52,704]{1,0:T(8,128)S(1)}, u32[]{:S(2)}, u32[]{:S(2)}) %collective-permute-start.13) | collective-permute-done | bytes 146464 | tf_op jit(solution)/shard_map/ppermute | solution.py:60
  463.0 12.3 %fusion.99 = bf16[2,16,16,704]{3,2,1,0:T(8,128)(2,1)} fusion(f32[2,16,16,704]{3,2,1,0:T(8,128)S(1)} %bitcast.104, bf16[2,16,16,704]{3,2,1,0:T(8,128)(2,1)S(1)} %copy-done.2, f32[704]{0:T(1024)S(1)} %get-tuple-element.123, f32[704]{0:T(1024)S(1)} %get-tuple-element.124, f32[704]{0:T(1024)S(1)} %get-tuple-element.77, f32[704]{0:T(1024)S(1)} %get-tuple-element.78, ...), kind=kLoop, calls=%fused_computation.203 | loop fusion | flops 36044800 | bytes 3021568 | tf_op jit(solution)/shard_map/convert_element_type | solution.py:147
  476.6 3.7 convert_bitcast_fusion
  480.3 141.5 %reduce-scatter.3.cloned.1.call-done = bf16[352,2816]{1,0:T(8,128)(2,1)} async-done(((bf16[2816,2816]{1,0:T(8,128)(2,1)}), bf16[352,2816]{1,0:T(8,128)(2,1)}) %reduce-scatter.3.cloned.1.call-update) | async-done | bytes 1982480 | tf_op jit(solution)/shard_map/reduce_scatter | solution.py:53
  621.9 3.7 convert_element_type.89
  (160 shorter events, 46.8 us)
Async XLA Ops:
  7.2 1.6 copy-start.3
  7.2 148.8 %all-gather.3.cloned.1.call-start = ((), (), s32[]{:S(2)}) async-start(), calls=%async_computation.2 | async-start | bytes 17842176 | tf_op jit(solution)/shard_map/all_gather | solution.py:83
  7.9 291.6 %all-gather.5.cloned.1.call-start = ((), (), s32[]{:S(2)}) async-start(), calls=%async_computation.3 | async-start | bytes 17842176 | tf_op jit(solution)/shard_map/all_gather | solution.py:92
  8.7 0.9 copy-start.9
  8.7 467.9 %reduce-scatter.5.cloned.1.call-start = ((), (), s32[]{:S(2)}) async-start(), calls=%async_computation.5 | async-start | bytes 17842176 | tf_op jit(solution)/shard_map/reduce_scatter | solution.py:53
  22.3 19.9 %copy-start.10 = (f32[704]{0:T(1024)S(1)}, f32[704]{0:T(1024)}, u32[]{:S(2)}) copy-start(f32[704]{0:T(1024)} %param.10) | copy-start | bytes 8452
  22.3 19.9 %copy-start.12 = (f32[704]{0:T(1024)S(1)}, f32[704]{0:T(1024)}, u32[]{:S(2)}) copy-start(f32[704]{0:T(1024)} %param.11) | copy-start | bytes 8452
  42.1 5.0 copy-start.11
  45.6 19.4 %collective-permute-start = (bf16[512,704]{0,1:T(8,128)(2,1)}, bf16[512,704]{0,1:T(8,128)(2,1)}, u32[]{:S(2)}, u32[]{:S(2)}) collective-permute-start(bf16[512,704]{0,1:T(8,128)(2,1)} %copy.16), channel_id=1, source_target_pairs={{0,1},{1,0},{2,3},{3,2},{4,5},{5,4},{6,7},{7,6},{8,9},{9,8},{10,11... | collective-permute-start | bytes 2162696 | tf_op jit(solution)/shard_map/ppermute | solution.py:35
  51.5 46.0 %collective-permute-start.3 = (bf16[512,704]{0,1:T(8,128)(2,1)}, bf16[512,704]{0,1:T(8,128)(2,1)}, u32[]{:S(2)}, u32[]{:S(2)}) collective-permute-start(bf16[512,704]{0,1:T(8,128)(2,1)} %copy.22), channel_id=1, source_target_pairs={{0,1},{1,0},{2,3},{3,2},{4,5},{5,4},{6,7},{7,6},{8,9},{9,8},{10,11... | collective-permute-start | bytes 2162696 | tf_op jit(solution)/shard_map/ppermute | solution.py:35
  52.2 56.7 %collective-permute-start.1 = (bf16[512,704]{0,1:T(8,128)(2,1)}, bf16[512,704]{0,1:T(8,128)(2,1)}, u32[]{:S(2)}, u32[]{:S(2)}) collective-permute-start(bf16[512,704]{0,1:T(8,128)(2,1)} %copy.16), channel_id=1, source_target_pairs={{0,2},{1,3},{2,0},{3,1},{4,6},{5,7},{6,4},{7,5},{8,10},{9,11},{10,... | collective-permute-start | bytes 2162696 | tf_op jit(solution)/shard_map/ppermute | solution.py:35
  52.7 66.5 %collective-permute-start.4 = (bf16[512,704]{0,1:T(8,128)(2,1)}, bf16[512,704]{0,1:T(8,128)(2,1)}, u32[]{:S(2)}, u32[]{:S(2)}) collective-permute-start(bf16[512,704]{0,1:T(8,128)(2,1)} %copy.22), channel_id=1, source_target_pairs={{0,2},{1,3},{2,0},{3,1},{4,6},{5,7},{6,4},{7,5},{8,10},{9,11},{10,... | collective-permute-start | bytes 2162696 | tf_op jit(solution)/shard_map/ppermute | solution.py:35
  54.2 75.3 %collective-permute-start.2 = (bf16[512,704]{0,1:T(8,128)(2,1)}, bf16[512,704]{0,1:T(8,128)(2,1)}, u32[]{:S(2)}, u32[]{:S(2)}) collective-permute-start(bf16[512,704]{0,1:T(8,128)(2,1)} %copy.16), channel_id=1, source_target_pairs={{0,3},{1,2},{2,1},{3,0},{4,7},{5,6},{6,5},{7,4},{8,11},{9,10},{10,... | collective-permute-start | bytes 2162696 | tf_op jit(solution)/shard_map/ppermute | solution.py:35
  65.0 75.1 %collective-permute-start.5 = (bf16[512,704]{0,1:T(8,128)(2,1)}, bf16[512,704]{0,1:T(8,128)(2,1)}, u32[]{:S(2)}, u32[]{:S(2)}) collective-permute-start(bf16[512,704]{0,1:T(8,128)(2,1)} %copy.22), channel_id=1, source_target_pairs={{0,3},{1,2},{2,1},{3,0},{4,7},{5,6},{6,5},{7,4},{8,11},{9,10},{10,... | collective-permute-start | bytes 2162696 | tf_op jit(solution)/shard_map/ppermute | solution.py:35
  156.0 16.8 %copy-start.7 = (bf16[512,2816]{1,0:T(8,128)(2,1)S(1)}, bf16[512,2816]{1,0:T(8,128)(2,1)}, u32[]{:S(2)}) copy-start(bf16[512,2816]{1,0:T(8,128)(2,1)} %dynamic_update_slice.31) | copy-start | bytes 8650756
  171.2 1.6 copy-start.13
  299.5 322.4 %reduce-scatter.3.cloned.1.call-start = ((), (), s32[]{:S(2)}) async-start(), calls=%async_computation.4 | async-start | bytes 17842176 | tf_op jit(solution)/shard_map/reduce_scatter | solution.py:53
  299.5 16.8 %copy-start.8 = (bf16[512,2816]{1,0:T(8,128)(2,1)S(1)}, bf16[512,2816]{1,0:T(8,128)(2,1)}, u32[]{:S(2)}) copy-start(bf16[512,2816]{1,0:T(8,128)(2,1)} %dynamic_update_slice.27) | copy-start | bytes 8650756
  314.8 1.5 copy-start.14
  342.1 2.8 copy-start.5
  351.7 34.7 %collective-permute-start.7 = (bf16[512,704]{0,1:T(8,128)(2,1)}, bf16[512,704]{0,1:T(8,128)(2,1)}, u32[]{:S(2)}, u32[]{:S(2)}) collective-permute-start(bf16[512,704]{0,1:T(8,128)(2,1)} %copy.30), channel_id=1, source_target_pairs={{0,2},{1,3},{2,0},{3,1},{4,6},{5,7},{6,4},{7,5},{8,10},{9,11},{10,... | collective-permute-start | bytes 2162696 | tf_op jit(solution)/shard_map/ppermute | solution.py:48
  353.2 37.0 %collective-permute-start.8 = (bf16[512,704]{0,1:T(8,128)(2,1)}, bf16[512,704]{0,1:T(8,128)(2,1)}, u32[]{:S(2)}, u32[]{:S(2)}) collective-permute-start(bf16[512,704]{0,1:T(8,128)(2,1)} %copy.32), channel_id=1, source_target_pairs={{0,3},{1,2},{2,1},{3,0},{4,7},{5,6},{6,5},{7,4},{8,11},{9,10},{10,... | collective-permute-start | bytes 2162696 | tf_op jit(solution)/shard_map/ppermute | solution.py:48
  354.6 37.8 %collective-permute-start.6 = (bf16[512,704]{0,1:T(8,128)(2,1)}, bf16[512,704]{0,1:T(8,128)(2,1)}, u32[]{:S(2)}, u32[]{:S(2)}) collective-permute-start(bf16[512,704]{0,1:T(8,128)(2,1)} %copy.28), channel_id=1, source_target_pairs={{0,1},{1,0},{2,3},{3,2},{4,5},{5,4},{6,7},{7,6},{8,9},{9,8},{10,11... | collective-permute-start | bytes 2162696 | tf_op jit(solution)/shard_map/ppermute | solution.py:48
  368.7 2.8 copy-start.6
  376.1 40.5 %collective-permute-start.10 = (bf16[512,704]{0,1:T(8,128)(2,1)}, bf16[512,704]{0,1:T(8,128)(2,1)}, u32[]{:S(2)}, u32[]{:S(2)}) collective-permute-start(bf16[512,704]{0,1:T(8,128)(2,1)} %copy.36), channel_id=1, source_target_pairs={{0,2},{1,3},{2,0},{3,1},{4,6},{5,7},{6,4},{7,5},{8,10},{9,11},{10,... | collective-permute-start | bytes 2162696 | tf_op jit(solution)/shard_map/ppermute | solution.py:48
  379.9 39.1 %collective-permute-start.11 = (bf16[512,704]{0,1:T(8,128)(2,1)}, bf16[512,704]{0,1:T(8,128)(2,1)}, u32[]{:S(2)}, u32[]{:S(2)}) collective-permute-start(bf16[512,704]{0,1:T(8,128)(2,1)} %copy.38), channel_id=1, source_target_pairs={{0,3},{1,2},{2,1},{3,0},{4,7},{5,6},{6,5},{7,4},{8,11},{9,10},{10,... | collective-permute-start | bytes 2162696 | tf_op jit(solution)/shard_map/ppermute | solution.py:48
  386.4 34.8 %collective-permute-start.9 = (bf16[512,704]{0,1:T(8,128)(2,1)}, bf16[512,704]{0,1:T(8,128)(2,1)}, u32[]{:S(2)}, u32[]{:S(2)}) collective-permute-start(bf16[512,704]{0,1:T(8,128)(2,1)} %copy.34), channel_id=1, source_target_pairs={{0,1},{1,0},{2,3},{3,2},{4,5},{5,4},{6,7},{7,6},{8,9},{9,8},{10,11... | collective-permute-start | bytes 2162696 | tf_op jit(solution)/shard_map/ppermute | solution.py:48
  445.5 4.4 copy-start
  445.7 4.2 copy-start.4
  452.8 10.2 %copy-start.1 = (f32[512,704]{1,0:T(8,128)S(1)}, f32[512,704]{1,0:T(8,128)}, u32[]{:S(2)}) copy-start(f32[512,704]{1,0:T(8,128)} %copy-done) | copy-start | bytes 4325380
  452.8 10.2 %copy-start.2 = (bf16[2,16,16,704]{3,2,1,0:T(8,128)(2,1)S(1)}, bf16[2,16,16,704]{3,2,1,0:T(8,128)(2,1)}, u32[]{:S(2)}) copy-start(bf16[2,16,16,704]{3,2,1,0:T(8,128)(2,1)} %param.15) | copy-start | bytes 2162692
  453.7 1.5 collective-permute-start.12
  455.2 6.7 %collective-permute-start.13 = (f32[52,704]{1,0:T(8,128)S(1)}, f32[52,704]{1,0:T(8,128)S(1)}, u32[]{:S(2)}, u32[]{:S(2)}) collective-permute-start(f32[52,704]{1,0:T(8,128)S(1)} %fusion.121), channel_id=1, source_target_pairs={{0,8},{4,12},{8,0},{12,4},{16,24},{20,28},{24,16},{28,20},{1,9},{5... | collective-permute-start | bytes 439304 | tf_op jit(solution)/shard_map/ppermute | solution.py:60
  461.9 13.4 %collective-permute-start.14 = (f32[52,704]{1,0:T(8,128)S(1)}, f32[52,704]{1,0:T(8,128)S(1)}, u32[]{:S(2)}, u32[]{:S(2)}) collective-permute-start(f32[52,704]{1,0:T(8,128)S(1)} %add.498), channel_id=1, source_target_pairs={{0,16},{4,20},{8,24},{12,28},{16,0},{20,4},{24,8},{28,12},{1,17},{... | collective-permute-start | bytes 439304 | tf_op jit(solution)/shard_map/ppermute | solution.py:60
Sparse Core Ops, SparseCore 0:
  9.7 146.2 all-gather.2
  157.6 141.8 all-gather.4
  301.8 157.9 reduce-scatter.4
  462.0 159.8 reduce-scatter.2

commit v2 on v1

--- a/solution.py
+++ b/solution.py
@@ -51,6 +51,32 @@
 
 def dp_scatter(partial):
     return lax.psum_scatter(partial, "dp", scatter_dimension=0, tiled=True)
+
+
+def dp_line_scatter(partial, early):
+    n = lax.axis_size("dp")
+    m = n // 2
+    me = lax.axis_index("dp")
+    place, side = me // 2, me % 2
+    blocks = partial.reshape(m, 2, partial.shape[0] // n, partial.shape[1])
+    own = lax.dynamic_index_in_dim(blocks, side, 1, keepdims=False)
+    other = lax.dynamic_index_in_dim(blocks, 1 - side, 1, keepdims=False)
+    own = own + lax.ppermute(other, "dp", swap_pairs(1, n))
+    up = down = None
+    for distance in range(m - 1, 0, -1):
+        high = lax.dynamic_index_in_dim(
+            own, jnp.minimum(place + distance, m - 1), 0, keepdims=False
+        )
+        low = lax.dynamic_index_in_dim(own, jnp.maximum(place - distance, 0), 0, keepdims=False)
+        if up is not None:
+            high, low = high + up, low + down
+        senders = range(2 * (m - distance))
+        up = lax.ppermute(high, "dp", [(i, i + 2) for i in senders])
+        down = lax.ppermute(low, "dp", [(n - 1 - i, n - 3 - i) for i in senders])
+        if distance == 2:
+            up, down, early = lax.optimization_barrier((up, down, early))
+    mine = lax.dynamic_index_in_dim(own, place, 0, keepdims=False).astype(jnp.float32)
+    return mine + up.astype(jnp.float32) + down.astype(jnp.float32), early
 
 
 def dp_total(value):
@@ -90,8 +116,8 @@
         dbranch_all, hidden, (((0,), (0,)), ((), ())), preferred_element_type=jnp.float32
     ).astype(jnp.bfloat16)
     reduce_all = lax.all_gather(w_reduce, "dp", axis=1, tiled=True)
-    reduce_part, reduce_all = lax.optimization_barrier((reduce_part, reduce_all))
-    grad_reduce = dp_scatter(reduce_part).astype(jnp.float32).T
+    grad_reduce, reduce_all = dp_line_scatter(reduce_part, reduce_all)
+    grad_reduce = grad_reduce.T
     dhidden = lax.dot_general(
         dbranch_all, reduce_all, (((1,), (1,)), ((), ())), preferred_element_type=jnp.float32
     )

time: 644 us -> 652 us (1.012)
  starting transfers between devices: 16.4 us -> 36.4 us
  other arithmetic: 54.9 us -> 72.9 us
  waiting for transfers between devices: 307 us -> 289 us
  local copies, waits for them, and re-layouts: 128 us -> 121 us
    reduce_scatter x2 -> x1, waiting for transfers between devices: 142 us -> 0.01 us  [dp_scatter(): return lax.psum_scatter(partial, 'dp', scatter_dimension=0, tiled=True)]
    ppermute x0 -> x7, waiting for transfers between devices: none -> 117 us  [the longest x3 104 us: dp_line_scatter(): up = lax.ppermute(high, 'dp', [(i, i + 2) for i in senders])]
    all_gather x1, waiting for transfers between devices: 115 us -> 44.4 us  [body(): reduce_all = lax.all_gather(w_reduce, 'dp', axis=1, tiled=True)]
    ppermute x3, waiting for transfers between devices: 8.01 us -> 73.4 us  [dp_total(): value = value + lax.ppermute(value, 'dp', swap_pairs(shift, n))]
    ppermute x0 -> x7, starting transfers between devices: none -> 17.4 us  [the longest x3 13 us: dp_line_scatter(): up = lax.ppermute(high, 'dp', [(i, i + 2) for i in senders])]
    add x0 -> x3, other arithmetic: none -> 17.2 us  [the longest x2 10.9 us: dp_line_scatter(): high, low = (high + up, low + down)]
    squeeze x0 -> x2, local copies, waits for them, and re-layouts: none -> 9.35 us  [the longest x1 6.96 us: dp_line_scatter(): other = lax.dynamic_index_in_dim(blocks, 1 - side, 1, keepdims=False)]
    all_gather x1, waiting for transfers between devices: 5.22 us -> 12.4 us  [body(): expand_all = lax.all_gather(w_expand, 'dp', axis=0, tiled=True)]
  transfers between devices with their start and end apart: 19 -> 25, of which waited for: 8 -> 10; matrix products, arithmetic and copies ran while one was open for 41% -> 37% of each run, Pallas kernels for 0% -> 0%
where the time goes in v2:
time: 652 us; the launch traced here: 646 us
  waiting for transfers between devices  289 us (44%)
  local copies, waits for them, and re-layouts  121 us (19%)
  matrix products  82 us (13%)
  other arithmetic  72.9 us (11%)
  starting transfers between devices  36.4 us (6%)
  blocking collectives  28.7 us (4%)
  between operations  16.1 us (2%)
    ppermute x3, waiting for transfers between devices, dp_line_scatter(): up = lax.ppermute(high, 'dp', [(i, i + 2) for i in senders])  104 us
    ppermute x3, waiting for transfers between devices, dp_total(): value = value + lax.ppermute(value, 'dp', swap_pairs(shift, n))  73.4 us
    dynamic_update_slice x8, local copies, waits for them, and re-layouts, chan_gather(): whole = lax.dynamic_update_slice(whole, parts[k], (0, (me ^ k) * width))  64.5 us
    all_gather x1, waiting for transfers between devices, body(): reduce_all = lax.all_gather(w_reduce, 'dp', axis=1, tiled=True)  44.4 us
    ppermute x6, waiting for transfers between devices, chan_scatter(): lax.ppermute(mine, 'chan', swap_pairs(k, n)).astype(jnp.float32)  28.1 us
    dot_general x1, matrix products, body(): lax.dot_general(dbranch_all, reduce_all, (((1,), (1,)), ((), ())), prefer...  15.4 us
    dot_general x1, matrix products, body(): pre = jnp.dot(normed_all, expand_all, preferred_element_type=jnp.float32)  15.2 us
    dot_general x1, matrix products, body(): lax.dot_general(dpre, expand_all, (((1,), (1,)), ((), ())), preferred_ele...  13.6 us
  transfers between devices with their start and end apart: 25, of which 10 were waited for; matrix products, arithmetic and copies ran while one was open for 37% of the time, Pallas kernels for 0%

profile of v2, /device:TPU:0, one launch (start us, length us, event | category | flops | bytes accessed | tf_op | source)
XLA Modules:
  0.0 646.5 jit_solution(1714485748534928411)
XLA Ops:
  11.0 13.1 %fusion.110 = (f32[2,16,16]{2,1,0:T(8,128)S(1)}, f32[2,16,16,704]{3,2,1,0:T(8,128)S(1)}) fusion(f32[704]{0:T(1024)S(1)} %get-tuple-element.125, f32[704]{0:T(1024)S(1)} %get-tuple-element.126, f32[704]{0:T(1024)S(1)} %get-tuple-element.79, f32[704]{0:T(1024)S(1)} %get-tuple-element.80, f32[704]{0:T(1024)S(1)} %get-tuple-element.81, ...), kind=kLoop, calls=%fused_computation.354 | loop fusion | flops 35323392 | bytes 3023616 | tf_op jit(solution)/shard_map/reduce_sum | solution.py:102
  24.6 11.3 %psum.28 = f32[512]{0:T(512)S(1)} all-reduce(f32[512]{0:T(512)S(1)} %reduce_sum.509), channel_id=1, replica_groups=mesh['dp'=8,'chan'=4] {'chan'}, use_global_device_ids=true, to_apply=%region_1.2 | all-reduce | flops 512 | bytes 4096 | tf_op jit(solution)/shard_map/psum | solution.py:102
  36.4 8.2 %psum.29 = f32[512]{0:T(512)S(1)} all-reduce(f32[512]{0:T(512)S(1)} %reduce_sum.511), channel_id=1, replica_groups=mesh['dp'=8,'chan'=4] {'chan'}, use_global_device_ids=true, to_apply=%region_3.4 | all-reduce | flops 512 | bytes 4096 | tf_op jit(solution)/shard_map/psum | solution.py:104
  53.1 12.5 %collective-permute-done = bf16[512,704]{0,1:T(8,128)(2,1)} collective-permute-done((bf16[512,704]{0,1:T(8,128)(2,1)}, bf16[512,704]{0,1:T(8,128)(2,1)}, u32[]{:S(2)}, u32[]{:S(2)}) %collective-permute-start) | collective-permute-done | bytes 720928 | tf_op jit(solution)/shard_map/ppermute | solution.py:35
  68.9 7.8 %dynamic_update_slice.24 = bf16[512,2816]{1,0:T(8,128)(2,1)} dynamic-update-slice(bf16[512,2816]{1,0:T(8,128)(2,1)} %broadcast.41.clone, bf16[512,704]{1,0:T(8,128)(2,1)S(1)} %copy-done.10, s32[]{:T(128)} %constant.80.clone.1, s32[]{:T(128)S(6)} %select_n.58) | dynamic-update-slice | bytes 1441796 | tf_op jit(solution)/shard_map/dynamic_update_slice | solution.py:37
  78.5 7.8 %dynamic_update_slice.28 = bf16[512,2816]{1,0:T(8,128)(2,1)} dynamic-update-slice(bf16[512,2816]{1,0:T(8,128)(2,1)} %broadcast.41.clone.1, bf16[512,704]{1,0:T(8,128)(2,1)S(1)} %fusion.106, s32[]{:T(128)} %constant.80.clone.1, s32[]{:T(128)S(6)} %select_n.58) | dynamic-update-slice | bytes 1441796 | tf_op jit(solution)/shard_map/dynamic_update_slice | solution.py:37
  87.7 8.7 %dynamic_update_slice.25 = bf16[512,2816]{1,0:T(8,128)(2,1)} dynamic-update-slice(bf16[512,2816]{1,0:T(8,128)(2,1)} %dynamic_update_slice.24, bf16[512,704]{1,0:T(8,128)(2,1)S(1)} %copy.17, s32[]{:T(128)} %constant.80.clone.1, s32[]{:T(128)S(6)} %select_n.59) | dynamic-update-slice | bytes 1441796 | tf_op jit(solution)/shard_map/dynamic_update_slice | solution.py:37
  97.7 8.7 %dynamic_update_slice.29 = bf16[512,2816]{1,0:T(8,128)(2,1)} dynamic-update-slice(bf16[512,2816]{1,0:T(8,128)(2,1)} %dynamic_update_slice.28, bf16[512,704]{1,0:T(8,128)(2,1)S(1)} %copy.23, s32[]{:T(128)} %constant.80.clone.1, s32[]{:T(128)S(6)} %select_n.59) | dynamic-update-slice | bytes 1441796 | tf_op jit(solution)/shard_map/dynamic_update_slice | solution.py:37
  107.8 7.8 %dynamic_update_slice.26 = bf16[512,2816]{1,0:T(8,128)(2,1)} dynamic-update-slice(bf16[512,2816]{1,0:T(8,128)(2,1)} %dynamic_update_slice.25, bf16[512,704]{1,0:T(8,128)(2,1)S(1)} %copy.19, s32[]{:T(128)} %constant.80.clone.1, s32[]{:T(128)S(6)} %select_n.60) | dynamic-update-slice | bytes 1441796 | tf_op jit(solution)/shard_map/dynamic_update_slice | solution.py:37
  117.0 7.8 %dynamic_update_slice.30 = bf16[512,2816]{1,0:T(8,128)(2,1)} dynamic-update-slice(bf16[512,2816]{1,0:T(8,128)(2,1)} %dynamic_update_slice.29, bf16[512,704]{1,0:T(8,128)(2,1)S(1)} %copy.25, s32[]{:T(128)} %constant.80.clone.1, s32[]{:T(128)S(6)} %select_n.60) | dynamic-update-slice | bytes 1441796 | tf_op jit(solution)/shard_map/dynamic_update_slice | solution.py:37
  126.2 8.0 %dynamic_update_slice.27 = bf16[512,2816]{1,0:T(8,128)(2,1)} dynamic-update-slice(bf16[512,2816]{1,0:T(8,128)(2,1)} %dynamic_update_slice.26, bf16[512,704]{1,0:T(8,128)(2,1)S(1)} %copy.21, s32[]{:T(128)} %constant.80.clone.1, s32[]{:T(128)S(6)} %select_n.61) | dynamic-update-slice | bytes 1441796 | tf_op jit(solution)/shard_map/dynamic_update_slice | solution.py:37
  135.6 8.0 %dynamic_update_slice.31 = bf16[512,2816]{1,0:T(8,128)(2,1)} dynamic-update-slice(bf16[512,2816]{1,0:T(8,128)(2,1)} %dynamic_update_slice.30, bf16[512,704]{1,0:T(8,128)(2,1)S(1)} %copy.27, s32[]{:T(128)} %constant.80.clone.1, s32[]{:T(128)S(6)} %select_n.61) | dynamic-update-slice | bytes 1441796 | tf_op jit(solution)/shard_map/dynamic_update_slice | solution.py:37
  143.6 12.4 %all-gather.3.cloned.1.call-done = bf16[2816,2816]{1,0:T(8,128)(2,1)} async-done(((bf16[352,2816]{1,0:T(8,128)(2,1)}), bf16[2816,2816]{1,0:T(8,128)(2,1)}) %all-gather.3.cloned.1.call-update) | async-done | bytes 15859728 | tf_op jit(solution)/shard_map/all_gather | solution.py:109
  156.0 15.2 %multiply_convert_fusion = (bf16[512,2816]{1,0:T(8,128)(2,1)S(1)}, f32[512,2816]{1,0:T(8,128)}) fusion(bf16[512,2816]{1,0:T(8,128)(2,1)} %dynamic_update_slice.27, bf16[2816,2816]{1,0:T(8,128)(2,1)} %all-gather.3.cloned.1.call-done), kind=kOutput, calls=%fused_computation.107 | convolution fusion | flops 8127381504 | bytes 27394048 | tf_op jit(solution)/shard_map/dot_general | solution.py:110
  171.2 12.4 %convolution_convert_fusion.1 = bf16[2816,2816]{1,0:T(8,128)(2,1)} fusion(bf16[512,2816]{1,0:T(8,128)(2,1)S(1)} %copy-done.13, bf16[512,2816]{1,0:T(8,128)(2,1)S(1)} %get-tuple-element.16), kind=kOutput, calls=%fused_computation.97 | convolution fusion | flops 8128102400 | bytes 21626880 | tf_op jit(solution)/shard_map/dot_general | solution.py:115
  183.5 7.0 %dynamic-slice_bitcast_fusion = bf16[4,352,2816]{2,1,0:T(8,128)(2,1)} fusion(bf16[4,2,352,2816]{3,2,1,0:T(8,128)(2,1)} %bitcast.125, s32[]{:T(128)S(6)} %select_n.64), kind=kLoop, calls=%fused_computation.100 | loop fusion | bytes 15859716 | tf_op jit(solution)/shard_map/jit(dynamic_index_in_dim)/squeeze | solution.py:63
  190.8 13.3 %collective-permute-done.6 = bf16[4,352,2816]{2,1,0:T(8,128)(2,1)} collective-permute-done((bf16[4,352,2816]{2,1,0:T(8,128)(2,1)}, bf16[4,352,2816]{2,1,0:T(8,128)(2,1)}, u32[]{:S(2)}, u32[]{:S(2)}) %collective-permute-start.6) | collective-permute-done | bytes 7929888 | tf_op jit(solution)/shard_map/ppermute | solution.py:64
  204.1 6.3 bitcast_add_fusion
  210.4 2.4 dynamic-slice_bitcast_fusion.1
  218.2 84.1 %collective-permute-done.7 = bf16[352,2816]{1,0:T(8,128)(2,1)S(1)} collective-permute-done((bf16[352,2816]{1,0:T(8,128)(2,1)}, bf16[352,2816]{1,0:T(8,128)(2,1)S(1)}, u32[]{:S(2)}, u32[]{:S(2)}) %collective-permute-start.7) | collective-permute-done | bytes 1982496 | tf_op jit(solution)/shard_map/ppermute | solution.py:74
  302.2 5.1 bitcast_add_fusion.3
  308.1 6.1 collective-permute-start.8
  314.2 44.4 %all-gather.5.cloned.1.call-done = bf16[2816,2816]{0,1:T(8,128)(2,1)} async-done(((bf16[2816,352]{0,1:T(8,128)(2,1)}), bf16[2816,2816]{0,1:T(8,128)(2,1)}) %all-gather.5.cloned.1.call-update) | async-done | bytes 15859728 | tf_op jit(solution)/shard_map/all_gather | solution.py:118
  358.6 19.9 %collective-permute-done.8 = bf16[352,2816]{1,0:T(8,128)(2,1)} collective-permute-done((bf16[352,2816]{1,0:T(8,128)(2,1)}, bf16[352,2816]{1,0:T(8,128)(2,1)}, u32[]{:S(2)}, u32[]{:S(2)}) %collective-permute-start.8) | collective-permute-done | bytes 1982496 | tf_op jit(solution)/shard_map/ppermute | solution.py:74
  378.5 15.4 %fusion.5 = bf16[512,2816]{1,0:T(8,128)(2,1)S(1)} fusion(f32[512,2816]{1,0:T(8,128)} %get-tuple-element.148, bf16[512,2816]{1,0:T(8,128)(2,1)} %dynamic_update_slice.31, bf16[2816,2816]{0,1:T(8,128)(2,1)} %all-gather.5.cloned.1.call-done), kind=kOutput, calls=%fused_computation.106 | convolution fusion | flops 8134590464 | bytes 27394048 | tf_op jit(solution)/shard_map/dot_general | solution.py:121
  395.5 11.8 %convolution_convert_fusion = bf16[2816,2816]{1,0:T(8,128)(2,1)} fusion(bf16[512,2816]{1,0:T(8,128)(2,1)S(1)} %copy-done.14, bf16[512,2816]{1,0:T(8,128)(2,1)S(1)} %fusion.5), kind=kOutput, calls=%fused_computation.96 | convolution fusion | flops 8128102400 | bytes 21626880 | tf_op jit(solution)/shard_map/dot_general | solution.py:126
  407.4 13.6 %convolution_convert_fusion.2 = bf16[512,2816]{1,0:T(8,128)(2,1)S(1)} fusion(bf16[512,2816]{1,0:T(8,128)(2,1)} %copy-done.103, bf16[2816,2816]{1,0:T(8,128)(2,1)} %all-gather.3.cloned.1.call-done), kind=kOutput, calls=%fused_computation.109 | convolution fusion | flops 8121614336 | bytes 21626880 | tf_op jit(solution)/shard_map/dot_general | solution.py:133
  423.2 2.3 copy.34
  431.3 13.5 %convolution_convert_fusion.3 = bf16[512,2816]{1,0:T(8,128)(2,1)S(1)} fusion(bf16[512,2816]{1,0:T(8,128)(2,1)} %copy-done.102, bf16[2816,2816]{0,1:T(8,128)(2,1)} %all-gather.5.cloned.1.call-done), kind=kOutput, calls=%fused_computation.110 | convolution fusion | flops 8121614336 | bytes 21626880 | tf_op jit(solution)/shard_map/dot_general | solution.py:137
  455.1 2.3 copy.35
  457.4 5.5 collective-permute-done.15
  462.9 2.3 copy.37
  465.2 2.3 copy.39
  467.5 8.3 %collective-permute-done.11 = bf16[512,704]{0,1:T(8,128)(2,1)} collective-permute-done((bf16[512,704]{0,1:T(8,128)(2,1)}, bf16[512,704]{0,1:T(8,128)(2,1)}, u32[]{:S(2)}, u32[]{:S(2)}) %collective-permute-start.11) | collective-permute-done | bytes 720928 | tf_op jit(solution)/shard_map/ppermute | solution.py:48
  475.8 2.3 copy.29
  478.1 14.3 %collective-permute-done.12 = bf16[512,704]{0,1:T(8,128)(2,1)S(1)} collective-permute-done((bf16[512,704]{0,1:T(8,128)(2,1)}, bf16[512,704]{0,1:T(8,128)(2,1)S(1)}, u32[]{:S(2)}, u32[]{:S(2)}) %collective-permute-start.12) | collective-permute-done | bytes 720928 | tf_op jit(solution)/shard_map/ppermute | solution.py:48
  494.7 5.7 fusion.107
  500.4 9.2 %all-reduce.2 = (f32[512]{0:T(512)S(1)}, f32[512]{0:T(512)S(1)}) all-reduce(f32[512]{0:T(512)S(1)} %get-tuple-element.151, f32[512]{0:T(512)S(1)} %get-tuple-element.150), channel_id=1, replica_groups=mesh['dp'=8,'chan'=4] {'chan'}, use_global_device_ids=true, to_apply=%region_7.8 | all-reduce | flops 1024 | bytes 8192 | tf_op jit(solution)/shard_map/psum | solution.py:145
  509.6 6.5 %multiply_reduce_fusion.2 = (f32[704]{0:T(1024)S(1)}, f32[704]{0:T(1024)S(1)}, f32[704]{0:T(1024)S(1)}, f32[704]{0:T(1024)S(1)}, f32[704]{0:T(1024)S(1)}, /*inde...) fusion(f32[2,16,16,704]{3,2,1,0:T(8,128)S(1)} %copy-done.2, ...), kind=kLoop, calls=%fused_computation.228 | loop fusion | flops 15486592 | bytes 5828864 | tf_op jit(solution)/shard_map/reduce_sum | solution.py:166
  516.1 4.1 multiply_reduce_fusion.1
  520.3 2.8 multiply_reduce_fusion.3
  524.7 5.8 bitcast_add_fusion.2
  530.5 5.5 collective-permute-start.20
  537.4 2.7 collective-permute-start.18
  540.1 73.4 %collective-permute-done.18 = f32[52,704]{1,0:T(8,128)S(1)} collective-permute-done((f32[52,704]{1,0:T(8,128)S(1)}, f32[52,704]{1,0:T(8,128)S(1)}, u32[]{:S(2)}, u32[]{:S(2)}) %collective-permute-start.18) | collective-permute-done | bytes 146464 | tf_op jit(solution)/shard_map/ppermute | solution.py:86
  616.0 13.3 %fusion.101 = bf16[2,16,16,704]{3,2,1,0:T(8,128)(2,1)} fusion(f32[2,16,16,704]{3,2,1,0:T(8,128)S(1)} %bitcast.124, bf16[2,16,16,704]{3,2,1,0:T(8,128)(2,1)S(1)} %copy-done.6, f32[704]{0:T(1024)S(1)} %copy-done.40, f32[704]{0:T(1024)S(1)} %copy-done.42, f32[704]{0:T(1024)S(1)} %copy-done.46, f32[704]{0:T(1024)S(1)} %copy-done.48, f32[704]{0:T(1024)S(1)} %copy-done.50, ...), kind=kLoop, calls=%fused_computation.213 | loop fusion | flops 36044800 | bytes 3021568 | tf_op jit(solution)/shard_map/convert_element_type | solution.py:173
  630.6 5.3 fusion.7
  636.0 3.7 convert_element_type.100
  (354 shorter events, 60.1 us)
Async XLA Ops:
  7.2 148.8 %all-gather.3.cloned.1.call-start = ((), (), s32[]{:S(2)}) async-start(), calls=%async_computation.1 | async-start | bytes 17842176 | tf_op jit(solution)/shard_map/all_gather | solution.py:109
  7.9 350.7 %all-gather.5.cloned.1.call-start = ((), (), s32[]{:S(2)}) async-start(), calls=%async_computation.2 | async-start | bytes 17842176 | tf_op jit(solution)/shard_map/all_gather | solution.py:118
  8.7 627.3 %reduce-scatter.2.cloned.1.call-start = ((), (), s32[]{:S(2)}) async-start(), calls=%async_computation.3 | async-start | bytes 17842176 | tf_op jit(solution)/shard_map/reduce_scatter | solution.py:53
  46.2 19.4 %collective-permute-start = (bf16[512,704]{0,1:T(8,128)(2,1)}, bf16[512,704]{0,1:T(8,128)(2,1)}, u32[]{:S(2)}, u32[]{:S(2)}) collective-permute-start(bf16[512,704]{0,1:T(8,128)(2,1)} %copy.16), channel_id=1, source_target_pairs={{0,1},{1,0},{2,3},{3,2},{4,5},{5,4},{6,7},{7,6},{8,9},{9,8},{10,11... | collective-permute-start | bytes 2162696 | tf_op jit(solution)/shard_map/ppermute | solution.py:35
  49.0 47.4 %collective-permute-start.3 = (bf16[512,704]{0,1:T(8,128)(2,1)}, bf16[512,704]{0,1:T(8,128)(2,1)}, u32[]{:S(2)}, u32[]{:S(2)}) collective-permute-start(bf16[512,704]{0,1:T(8,128)(2,1)} %copy.22), channel_id=1, source_target_pairs={{0,1},{1,0},{2,3},{3,2},{4,5},{5,4},{6,7},{7,6},{8,9},{9,8},{10,11... | collective-permute-start | bytes 2162696 | tf_op jit(solution)/shard_map/ppermute | solution.py:35
  49.5 56.9 %collective-permute-start.1 = (bf16[512,704]{0,1:T(8,128)(2,1)}, bf16[512,704]{0,1:T(8,128)(2,1)}, u32[]{:S(2)}, u32[]{:S(2)}) collective-permute-start(bf16[512,704]{0,1:T(8,128)(2,1)} %copy.16), channel_id=1, source_target_pairs={{0,2},{1,3},{2,0},{3,1},{4,6},{5,7},{6,4},{7,5},{8,10},{9,11},{10,... | collective-permute-start | bytes 2162696 | tf_op jit(solution)/shard_map/ppermute | solution.py:35
  50.1 65.5 %collective-permute-start.4 = (bf16[512,704]{0,1:T(8,128)(2,1)}, bf16[512,704]{0,1:T(8,128)(2,1)}, u32[]{:S(2)}, u32[]{:S(2)}) collective-permute-start(bf16[512,704]{0,1:T(8,128)(2,1)} %copy.22), channel_id=1, source_target_pairs={{0,2},{1,3},{2,0},{3,1},{4,6},{5,7},{6,4},{7,5},{8,10},{9,11},{10,... | collective-permute-start | bytes 2162696 | tf_op jit(solution)/shard_map/ppermute | solution.py:35
  51.5 73.3 %collective-permute-start.2 = (bf16[512,704]{0,1:T(8,128)(2,1)}, bf16[512,704]{0,1:T(8,128)(2,1)}, u32[]{:S(2)}, u32[]{:S(2)}) collective-permute-start(bf16[512,704]{0,1:T(8,128)(2,1)} %copy.16), channel_id=1, source_target_pairs={{0,3},{1,2},{2,1},{3,0},{4,7},{5,6},{6,5},{7,4},{8,11},{9,10},{10,... | collective-permute-start | bytes 2162696 | tf_op jit(solution)/shard_map/ppermute | solution.py:35
  65.6 68.6 %collective-permute-start.5 = (bf16[512,704]{0,1:T(8,128)(2,1)}, bf16[512,704]{0,1:T(8,128)(2,1)}, u32[]{:S(2)}, u32[]{:S(2)}) collective-permute-start(bf16[512,704]{0,1:T(8,128)(2,1)} %copy.22), channel_id=1, source_target_pairs={{0,3},{1,2},{2,1},{3,0},{4,7},{5,6},{6,5},{7,4},{8,11},{9,10},{10,... | collective-permute-start | bytes 2162696 | tf_op jit(solution)/shard_map/ppermute | solution.py:35
  190.5 13.6 %collective-permute-start.6 = (bf16[4,352,2816]{2,1,0:T(8,128)(2,1)}, bf16[4,352,2816]{2,1,0:T(8,128)(2,1)}, u32[]{:S(2)}, u32[]{:S(2)}) collective-permute-start(bf16[4,352,2816]{2,1,0:T(8,128)(2,1)} %dynamic-slice_bitcast_fusion), channel_id=1, source_target_pairs={{0,4},{4,0},{8,12},{12,8},{16,20},{20,16},{24,28},{28,24},{1,5},{5... | collective-permute-start | bytes 23789576 | tf_op jit(solution)/shard_map/ppermute | solution.py:64
  214.8 87.5 %collective-permute-start.7 = (bf16[352,2816]{1,0:T(8,128)(2,1)}, bf16[352,2816]{1,0:T(8,128)(2,1)S(1)}, u32[]{:S(2)}, u32[]{:S(2)}) collective-permute-start(bf16[352,2816]{1,0:T(8,128)(2,1)} %get-tuple-element.138), channel_id=1, source_target_pairs={{0,8},{4,12},{1,9},{5,13},{2,10},{6,14},{3,11},{7,15}} | collective-permute-start | bytes 5947400 | tf_op jit(solution)/shard_map/ppermute | solution.py:74
  216.2 86.0 %collective-permute-start.9 = (bf16[352,2816]{1,0:T(8,128)(2,1)}, bf16[352,2816]{1,0:T(8,128)(2,1)}, u32[]{:S(2)}, u32[]{:S(2)}) collective-permute-start(bf16[352,2816]{1,0:T(8,128)(2,1)} %get-tuple-element.137), channel_id=1, source_target_pairs={{28,20},{24,16},{29,21},{25,17},{30,22},{26,18},{31,23},{27,19}} | collective-permute-start | bytes 5947400 | tf_op jit(solution)/shard_map/ppermute | solution.py:75
  307.3 51.3 %collective-permute-start.10 = (bf16[352,2816]{1,0:T(8,128)(2,1)}, bf16[352,2816]{1,0:T(8,128)(2,1)S(1)}, u32[]{:S(2)}, u32[]{:S(2)}) collective-permute-start(bf16[352,2816]{1,0:T(8,128)(2,1)} %get-tuple-element.135), channel_id=1, source_target_pairs={{28,20},{24,16},{20,12},{16,8},{29,21},{25,17},{21,13},{17,9},{30,... | collective-permute-start | bytes 5947400 | tf_op jit(solution)/shard_map/ppermute | solution.py:75
  308.1 70.4 %collective-permute-start.8 = (bf16[352,2816]{1,0:T(8,128)(2,1)}, bf16[352,2816]{1,0:T(8,128)(2,1)}, u32[]{:S(2)}, u32[]{:S(2)}) collective-permute-start(bf16[352,2816]{1,0:T(8,128)(2,1)} %get-tuple-element.136), channel_id=1, source_target_pairs={{0,8},{4,12},{8,16},{12,20},{1,9},{5,13},{9,17},{13,21},{2,10},{6,... | collective-permute-start | bytes 5947400 | tf_op jit(solution)/shard_map/ppermute | solution.py:74
  425.5 29.3 %collective-permute-start.14 = (bf16[512,704]{0,1:T(8,128)(2,1)}, bf16[512,704]{0,1:T(8,128)(2,1)}, u32[]{:S(2)}, u32[]{:S(2)}) collective-permute-start(bf16[512,704]{0,1:T(8,128)(2,1)} %copy.34), channel_id=1, source_target_pairs={{0,1},{1,0},{2,3},{3,2},{4,5},{5,4},{6,7},{7,6},{8,9},{9,8},{10,11... | collective-permute-start | bytes 2162696 | tf_op jit(solution)/shard_map/ppermute | solution.py:48
  428.4 34.5 %collective-permute-start.15 = (bf16[512,704]{0,1:T(8,128)(2,1)}, bf16[512,704]{0,1:T(8,128)(2,1)}, u32[]{:S(2)}, u32[]{:S(2)}) collective-permute-start(bf16[512,704]{0,1:T(8,128)(2,1)} %copy.36), channel_id=1, source_target_pairs={{0,2},{1,3},{2,0},{3,1},{4,6},{5,7},{6,4},{7,5},{8,10},{9,11},{10,... | collective-permute-start | bytes 2162696 | tf_op jit(solution)/shard_map/ppermute | solution.py:48
  431.0 34.2 %collective-permute-start.16 = (bf16[512,704]{0,1:T(8,128)(2,1)}, bf16[512,704]{0,1:T(8,128)(2,1)}, u32[]{:S(2)}, u32[]{:S(2)}) collective-permute-start(bf16[512,704]{0,1:T(8,128)(2,1)} %copy.38), channel_id=1, source_target_pairs={{0,3},{1,2},{2,1},{3,0},{4,7},{5,6},{6,5},{7,4},{8,11},{9,10},{10,... | collective-permute-start | bytes 2162696 | tf_op jit(solution)/shard_map/ppermute | solution.py:48
  449.3 26.5 %collective-permute-start.11 = (bf16[512,704]{0,1:T(8,128)(2,1)}, bf16[512,704]{0,1:T(8,128)(2,1)}, u32[]{:S(2)}, u32[]{:S(2)}) collective-permute-start(bf16[512,704]{0,1:T(8,128)(2,1)} %copy.28), channel_id=1, source_target_pairs={{0,1},{1,0},{2,3},{3,2},{4,5},{5,4},{6,7},{7,6},{8,9},{9,8},{10,11... | collective-permute-start | bytes 2162696 | tf_op jit(solution)/shard_map/ppermute | solution.py:48
  452.1 40.3 %collective-permute-start.12 = (bf16[512,704]{0,1:T(8,128)(2,1)}, bf16[512,704]{0,1:T(8,128)(2,1)S(1)}, u32[]{:S(2)}, u32[]{:S(2)}) collective-permute-start(bf16[512,704]{0,1:T(8,128)(2,1)} %copy.30), channel_id=1, source_target_pairs={{0,2},{1,3},{2,0},{3,1},{4,6},{5,7},{6,4},{7,5},{8,10},{9,11},{10,... | collective-permute-start | bytes 2162696 | tf_op jit(solution)/shard_map/ppermute | solution.py:48
  454.8 38.8 %collective-permute-start.13 = (bf16[512,704]{0,1:T(8,128)(2,1)}, bf16[512,704]{0,1:T(8,128)(2,1)S(1)}, u32[]{:S(2)}, u32[]{:S(2)}) collective-permute-start(bf16[512,704]{0,1:T(8,128)(2,1)} %copy.32), channel_id=1, source_target_pairs={{0,3},{1,2},{2,1},{3,0},{4,7},{5,6},{6,5},{7,4},{8,11},{9,10},{10,... | collective-permute-start | bytes 2162696 | tf_op jit(solution)/shard_map/ppermute | solution.py:48
  524.2 91.4 %copy-start.22 = (f32[704]{0:T(1024)S(1)}, f32[704]{0:T(1024)}, u32[]{:S(2)}) copy-start(f32[704]{0:T(1024)} %copy-done.21) | copy-start | bytes 8452
  524.2 91.4 %copy-start.24 = (f32[704]{0:T(1024)S(1)}, f32[704]{0:T(1024)}, u32[]{:S(2)}) copy-start(f32[704]{0:T(1024)} %copy-done.23) | copy-start | bytes 8452
  524.3 91.4 %copy-start.26 = (f32[704]{0:T(1024)S(1)}, f32[704]{0:T(1024)}, u32[]{:S(2)}) copy-start(f32[704]{0:T(1024)} %copy-done.25) | copy-start | bytes 8452
  524.3 91.4 %copy-start.28 = (f32[704]{0:T(1024)S(1)}, f32[704]{0:T(1024)}, u32[]{:S(2)}) copy-start(f32[704]{0:T(1024)} %copy-done.27) | copy-start | bytes 8452
  524.3 91.3 %copy-start.30 = (f32[704]{0:T(1024)S(1)}, f32[704]{0:T(1024)}, u32[]{:S(2)}) copy-start(f32[704]{0:T(1024)} %copy-done.29) | copy-start | bytes 8452
  524.3 91.3 %copy-start.32 = (f32[704]{0:T(1024)S(1)}, f32[704]{0:T(1024)}, u32[]{:S(2)}) copy-start(f32[704]{0:T(1024)} %copy-done.31) | copy-start | bytes 8452
  524.3 91.3 %copy-start.34 = (f32[704]{0:T(1024)S(1)}, f32[704]{0:T(1024)}, u32[]{:S(2)}) copy-start(f32[704]{0:T(1024)} %copy-done.33) | copy-start | bytes 8452
  524.3 91.3 %copy-start.36 = (f32[704]{0:T(1024)S(1)}, f32[704]{0:T(1024)}, u32[]{:S(2)}) copy-start(f32[704]{0:T(1024)} %copy-done.35) | copy-start | bytes 8452
  524.3 91.3 %copy-start.38 = (f32[704]{0:T(1024)S(1)}, f32[704]{0:T(1024)}, u32[]{:S(2)}) copy-start(f32[704]{0:T(1024)} %copy-done.37) | copy-start | bytes 8452
  524.3 91.3 %copy-start.40 = (f32[704]{0:T(1024)S(1)}, f32[704]{0:T(1024)}, u32[]{:S(2)}) copy-start(f32[704]{0:T(1024)} %copy-done.39) | copy-start | bytes 8452
  524.3 91.3 %copy-start.42 = (f32[704]{0:T(1024)S(1)}, f32[704]{0:T(1024)}, u32[]{:S(2)}) copy-start(f32[704]{0:T(1024)} %copy-done.41) | copy-start | bytes 8452
  524.3 91.3 %copy-start.44 = (f32[704]{0:T(1024)S(1)}, f32[704]{0:T(1024)}, u32[]{:S(2)}) copy-start(f32[704]{0:T(1024)} %copy-done.43) | copy-start | bytes 8452
  524.4 91.3 %copy-start.46 = (f32[704]{0:T(1024)S(1)}, f32[704]{0:T(1024)}, u32[]{:S(2)}) copy-start(f32[704]{0:T(1024)} %copy-done.45) | copy-start | bytes 8452
  524.4 91.3 %copy-start.48 = (f32[704]{0:T(1024)S(1)}, f32[704]{0:T(1024)}, u32[]{:S(2)}) copy-start(f32[704]{0:T(1024)} %copy-done.47) | copy-start | bytes 8452
  524.4 91.3 %copy-start.50 = (f32[704]{0:T(1024)S(1)}, f32[704]{0:T(1024)}, u32[]{:S(2)}) copy-start(f32[704]{0:T(1024)} %copy-done.49) | copy-start | bytes 8452
  524.4 91.3 %copy-start.52 = (f32[704]{0:T(1024)S(1)}, f32[704]{0:T(1024)}, u32[]{:S(2)}) copy-start(f32[704]{0:T(1024)} %copy-done.51) | copy-start | bytes 8452
  524.4 91.3 %copy-start.54 = (f32[704]{0:T(1024)S(1)}, f32[704]{0:T(1024)}, u32[]{:S(2)}) copy-start(f32[704]{0:T(1024)} %copy-done.53) | copy-start | bytes 8452
  524.4 91.3 %copy-start.56 = (f32[704]{0:T(1024)S(1)}, f32[704]{0:T(1024)}, u32[]{:S(2)}) copy-start(f32[704]{0:T(1024)} %copy-done.55) | copy-start | bytes 8452
  524.4 91.3 %copy-start.58 = (f32[704]{0:T(1024)S(1)}, f32[704]{0:T(1024)}, u32[]{:S(2)}) copy-start(f32[704]{0:T(1024)} %copy-done.57) | copy-start | bytes 8452
  524.4 91.3 %copy-start.60 = (f32[704]{0:T(1024)S(1)}, f32[704]{0:T(1024)}, u32[]{:S(2)}) copy-start(f32[704]{0:T(1024)} %copy-done.59) | copy-start | bytes 8452
  524.4 91.3 %copy-start.62 = (f32[704]{0:T(1024)S(1)}, f32[704]{0:T(1024)}, u32[]{:S(2)}) copy-start(f32[704]{0:T(1024)} %copy-done.61) | copy-start | bytes 8452
  524.4 91.3 %copy-start.64 = (f32[704]{0:T(1024)S(1)}, f32[704]{0:T(1024)}, u32[]{:S(2)}) copy-start(f32[704]{0:T(1024)} %copy-done.63) | copy-start | bytes 8452
  524.5 91.3 %copy-start.66 = (f32[704]{0:T(1024)S(1)}, f32[704]{0:T(1024)}, u32[]{:S(2)}) copy-start(f32[704]{0:T(1024)} %copy-done.65) | copy-start | bytes 8452
  524.6 12.8 %collective-permute-start.17 = (f32[52,704]{1,0:T(8,128)S(1)}, f32[52,704]{1,0:T(8,128)S(1)}, u32[]{:S(2)}, u32[]{:S(2)}) collective-permute-start(f32[52,704]{1,0:T(8,128)S(1)} %pad_maximum_fusion), channel_id=1, source_target_pairs={{0,4},{4,0},{8,12},{12,8},{16,20},{20,16},{24,28},{28,24},{1,5},{5... | collective-permute-start | bytes 439304 | tf_op jit(solution)/shard_map/ppermute | solution.py:86
  530.5 100.1 %collective-permute-start.20 = (bf16[352,2816]{1,0:T(8,128)(2,1)}, bf16[352,2816]{1,0:T(8,128)(2,1)}, u32[]{:S(2)}, u32[]{:S(2)}) collective-permute-start(bf16[352,2816]{1,0:T(8,128)(2,1)} %get-tuple-element.133), channel_id=1, source_target_pairs={{0,8},{4,12},{8,16},{12,20},{16,24},{20,28},{1,9},{5,13},{9,17},{1... | collective-permute-start | bytes 5947400 | tf_op jit(solution)/shard_map/ppermute | solution.py:74
  536.1 94.5 %collective-permute-start.21 = (bf16[352,2816]{1,0:T(8,128)(2,1)}, bf16[352,2816]{1,0:T(8,128)(2,1)}, u32[]{:S(2)}, u32[]{:S(2)}) collective-permute-start(bf16[352,2816]{1,0:T(8,128)(2,1)} %get-tuple-element.134), channel_id=1, source_target_pairs={{28,20},{24,16},{20,12},{16,8},{12,4},{8,0},{29,21},{25,17},{21,13... | collective-permute-start | bytes 5947400 | tf_op jit(solution)/shard_map/ppermute | solution.py:75
  537.4 76.1 %collective-permute-start.18 = (f32[52,704]{1,0:T(8,128)S(1)}, f32[52,704]{1,0:T(8,128)S(1)}, u32[]{:S(2)}, u32[]{:S(2)}) collective-permute-start(f32[52,704]{1,0:T(8,128)S(1)} %fusion.123), channel_id=1, source_target_pairs={{0,8},{4,12},{8,0},{12,4},{16,24},{20,28},{24,16},{28,20},{1,9},{5... | collective-permute-start | bytes 439304 | tf_op jit(solution)/shard_map/ppermute | solution.py:86
  613.5 15.7 %collective-permute-start.19 = (f32[52,704]{1,0:T(8,128)S(1)}, f32[52,704]{1,0:T(8,128)S(1)}, u32[]{:S(2)}, u32[]{:S(2)}) collective-permute-start(f32[52,704]{1,0:T(8,128)S(1)} %add.568), channel_id=1, source_target_pairs={{0,16},{4,20},{8,24},{12,28},{16,0},{20,4},{24,8},{28,12},{1,17},{... | collective-permute-start | bytes 439304 | tf_op jit(solution)/shard_map/ppermute | solution.py:86
  (81 other events, 2346.7 us)
Sparse Core Ops, SparseCore 0:
  9.7 146.2 all-gather.2
  157.6 200.9 all-gather.4
  407.5 188.7 reduce-scatter.1
